TPU v7x, 256 devices: a whole 4x4x8 slice. The times are simulated.
256 devices in a mesh: seq: 16 (over x, y), head: 16 (over z, core).
Axes of the slice: x: 4, y: 4, z: 8, core: 2. Of those that a mesh axis runs over, the one named last changes fastest.
Arguments:
- x_heads: bfloat16 [2, 4096, 16384], P(None, 'seq', 'head'), may hold values from -6 to 6
- gate_z: bfloat16 [2, 4096, 16384], P(None, 'seq', 'head'), may hold values from -6 to 6
- b_proj: bfloat16 [2, 4096, 128], P(None, 'seq'), may hold values from -0.59765625 to 0.59765625
- c_proj: bfloat16 [2, 4096, 128], P(None, 'seq'), may hold values from -6 to 6
- dt_raw: float32 [2, 4096, 256], P(None, 'seq', 'head'), may hold values from -3 to 3
- dt_bias: float32 [2, 256], P(None, 'head'), may hold values from -1 to 0.5
- decay_rate: float32 [2, 256], P(None, 'head'), may hold values from 0 to 1, as said below
- skip_d: float32 [2, 256], P(None, 'head'), may hold values from 0.5 to 1.5
- norm_gain: float32 [2, 16384], P(None, 'head'), may hold values from 0.5 to 1.5
- w_out: bfloat16 [2, 16384, 8192], P(None, 'head', 'seq'), may hold values from -0.046875 to 0.046875
- seg_ids: int32 [4096], P('seq'), may hold values from 0 to 8, never falling along the last dimension, each value on 1 to 1024 neighbouring positions
Outputs:
- mixed: bfloat16 [2, 4096, 8192], P(None, 'head', 'seq')
Inputs may be any that keep to these rules, and one draw needn't show every extreme that they name: `decay_rate`: Positive. `seg_ids`: document numbers start at 0, never fall along the sequence and take every value; one document has exactly 1024 tokens.
All inputs are finite; a program needn't handle non-finite values.
Results may differ from a plain program's by a relative error of at most 0.019.
Values may be sent and summed in bfloat16 or wider, within the bound.
A program may use at most 128 MiB of HBM per device.

v0:
```python
import jax
import jax.numpy as jnp
from jax import lax
from jax.sharding import PartitionSpec as P

HEADS = 256
HEADDIM = 64
SPAN = 256


highest = lax.Precision.HIGHEST


def passed_along(block, axis, distance):
    devices = range(lax.axis_size(axis))
    route = [(i - distance, i) for i in devices if i - distance in devices]
    return lax.ppermute(block, axis, route)


def to_blocks(tensor, nblocks):
    shaped = tensor.reshape(
        (tensor.shape[0], nblocks, tensor.shape[1] // nblocks) + tensor.shape[2:]
    )
    return jnp.moveaxis(shaped, 1, 0)


def from_blocks(tensor):
    moved = jnp.moveaxis(tensor, 0, 1)
    return moved.reshape((moved.shape[0], moved.shape[1] * moved.shape[2]) + moved.shape[3:])


def span_state(carried, before, offset, anchor, pieces):
    x_block, b_block, c_block, step_block, decay_block, seg_block = pieces
    running = jnp.cumsum(decay_block, axis=1)
    total = running[:, -1, :]
    kept = (seg_block == before).astype(jnp.float32)
    same_last = (seg_block == seg_block[-1]).astype(jnp.float32)
    tail_w = jnp.exp(total[:, None, :] - running) * same_last[None, :, None] * step_block
    fresh = jnp.einsum("mjh,mjhp,mjn->mhpn", tail_w, x_block, b_block, precision=highest)
    new_state = (jnp.exp(total) * kept[-1])[:, :, None, None] * carried + fresh
    factor = (
        jnp.exp(offset[:, None, :] + running)
        * (seg_block == anchor).astype(jnp.float32)[None, :, None]
    )
    return (new_state, factor, total)


def span_output(carried, before, pieces):
    x_block, b_block, c_block, step_block, decay_block, seg_block = pieces
    running = jnp.cumsum(decay_block, axis=1)
    kept = (seg_block == before).astype(jnp.float32)
    entry_w = jnp.exp(running) * kept[None, :, None]
    places = jnp.arange(seg_block.shape[0], dtype=jnp.int32)
    lower_mask = (places[:, None] >= places[None, :]) & (seg_block[:, None] == seg_block[None, :])
    run_t = jnp.transpose(running, (0, 2, 1))
    spread = run_t[:, :, :, None] - run_t[:, :, None, :]
    mixing = jnp.exp(jnp.minimum(spread, 0.0)) * lower_mask.astype(jnp.float32)
    products = jnp.einsum("min,mjn->mij", c_block, b_block, precision=highest)
    weights = mixing * products[:, None] * jnp.transpose(step_block, (0, 2, 1))[:, :, None, :]
    inside = jnp.einsum("mhij,mjhp->mihp", weights, x_block, precision=highest)
    entering = jnp.einsum("min,mhpn->mihp", c_block, carried, precision=highest)
    return inside + entry_w[..., None] * entering


def local(
    x_heads, gate_z, b_proj, c_proj, dt_raw, dt_bias, decay_rate, skip_d, norm_gain, w_out, seg_ids
):
    rows = x_heads.shape[1]
    local_heads = dt_raw.shape[2]
    head_size = x_heads.shape[2] // local_heads
    block = min(SPAN, rows)
    nblocks = rows // block
    step_size = jax.nn.softplus(dt_raw + dt_bias[:, None, :])
    log_decay = -decay_rate[:, None, :] * step_size
    x_float = x_heads.astype(jnp.float32).reshape(2, rows, local_heads, head_size)
    b_float = b_proj.astype(jnp.float32)
    c_float = c_proj.astype(jnp.float32)
    pieces = (
        to_blocks(x_float, nblocks),
        to_blocks(b_float, nblocks),
        to_blocks(c_float, nblocks),
        to_blocks(step_size, nblocks),
        to_blocks(log_decay, nblocks),
        seg_ids.reshape(nblocks, block),
    )
    anchor = passed_along(seg_ids[rows - 1 :], "seq", 1)[0]
    offset_zero = jnp.zeros((2, local_heads), jnp.float32)
    empty = jnp.zeros((2, local_heads, head_size, b_proj.shape[2]), jnp.float32)

    def joint_turn(carry, piece_set):
        carried, before, offset = carry
        output = span_output(carried, before, piece_set)
        new_state, factor, total = span_state(carried, before, offset, anchor, piece_set)
        return ((new_state, piece_set[5][-1], offset + total), (output, factor))

    ends, (outputs, factors) = lax.scan(joint_turn, (empty, anchor, offset_zero), pieces)
    local_state = ends[0]
    factor_all = from_blocks(factors)
    decay_dev = factor_all[:, -1, :]

    def relay_turn(counter, incoming):
        outgoing = local_state + decay_dev[:, :, None, None] * incoming
        return passed_along(outgoing.astype(jnp.bfloat16), "seq", 1).astype(outgoing.dtype)

    state_in = lax.fori_loop(0, lax.axis_size("seq") - 1, relay_turn, jnp.zeros_like(local_state))
    entering = jnp.einsum("mtn,mhpn->mthp", c_float, state_in, precision=highest)
    ssd_out = (
        from_blocks(outputs) + factor_all[..., None] * entering + skip_d[:, None, :, None] * x_float
    )
    gated = ssd_out.reshape(2, rows, local_heads * head_size) * jax.nn.silu(
        gate_z.astype(jnp.float32)
    )
    square_sum = lax.psum(jnp.sum(gated * gated, axis=2), "head")
    mean_square = square_sum / (HEADS * HEADDIM)
    normed = (gated * lax.rsqrt(mean_square + 1e-05)[:, :, None] * norm_gain[:, None, :]).astype(
        jnp.bfloat16
    )
    partial_terms = jnp.einsum(
        "mtk,mkd->mtd",
        lax.all_gather(normed, "seq", axis=1, tiled=True),
        w_out,
        preferred_element_type=jnp.float32,
    )
    summed = lax.psum_scatter(
        partial_terms.astype(jnp.bfloat16), "head", scatter_dimension=1, tiled=True
    )
    return summed


def solution(mesh):
    placed = (
        P(None, "seq", "head"),
        P(None, "seq", "head"),
        P(None, "seq", None),
        P(None, "seq", None),
        P(None, "seq", "head"),
        P(None, "head"),
        P(None, "head"),
        P(None, "head"),
        P(None, "head"),
        P(None, "head", "seq"),
        P("seq"),
    )
    return jax.shard_map(
        local, mesh=mesh, in_specs=placed, out_specs=P(None, "head", "seq"), check_vma=False
    )
```

profile of v0, /device:TPU:41, one launch (start us, length us, event | category | flops | bytes accessed | tf_op | source)
XLA Modules:
  0.0 558.1 jit_solution(7566085838849837888)
XLA Ops:
  30.6 252.5 %while.3 = (s32[]{:T(128)}, f32[2,16,64,128]{3,2,1,0:T(8,128)S(1)}, f32[2,1,16]{2,0,1:T(2,128)S(1)}, f32[2,16,64,128]{3,2,1,0:T(8,128)}, s32[]{:T(128)}, /*index=5*/s32[]{:T(128)}) while((s32[]{:T(128)}, f32[2,16,64,128]{3,2,1,0:T(8,128)S(1)}, f32[2,1,16]{2,0,1:T(2,128)S(1)}, f32[2,16,64,128]{3,2,1,0:T(8,128)}, s32[]{:T(128)}, ...), condition=%wide.region_3.4_spmd.clone, body=%wide.region_2.3_spmd.clone.sunk | while | flops 1310723 | bytes 6291703 | solution.py:105
  35.8 11.8 %collective-permute-done = bf16[2,16,64,128]{3,2,1,0:T(8,128)(2,1)} collective-permute-done((bf16[2,16,64,128]{3,2,1,0:T(8,128)(2,1)}, bf16[2,16,64,128]{3,2,1,0:T(8,128)(2,1)}, u32[]{:S(2)}, u32[]{:S(2)}) %collective-permute-start) | collective-permute-done | bytes 524320 | tf_op jit(solution)/shard_map/while/body/eval_jaxpr/ppermute | solution.py:17
  53.9 11.0 %collective-permute-done = bf16[2,16,64,128]{3,2,1,0:T(8,128)(2,1)} collective-permute-done((bf16[2,16,64,128]{3,2,1,0:T(8,128)(2,1)}, bf16[2,16,64,128]{3,2,1,0:T(8,128)(2,1)}, u32[]{:S(2)}, u32[]{:S(2)}) %collective-permute-start) | collective-permute-done | bytes 524320 | tf_op jit(solution)/shard_map/while/body/eval_jaxpr/ppermute | solution.py:17
  71.1 10.1 %collective-permute-done = bf16[2,16,64,128]{3,2,1,0:T(8,128)(2,1)} collective-permute-done((bf16[2,16,64,128]{3,2,1,0:T(8,128)(2,1)}, bf16[2,16,64,128]{3,2,1,0:T(8,128)(2,1)}, u32[]{:S(2)}, u32[]{:S(2)}) %collective-permute-start) | collective-permute-done | bytes 524320 | tf_op jit(solution)/shard_map/while/body/eval_jaxpr/ppermute | solution.py:17
  87.5 9.2 %collective-permute-done = bf16[2,16,64,128]{3,2,1,0:T(8,128)(2,1)} collective-permute-done((bf16[2,16,64,128]{3,2,1,0:T(8,128)(2,1)}, bf16[2,16,64,128]{3,2,1,0:T(8,128)(2,1)}, u32[]{:S(2)}, u32[]{:S(2)}) %collective-permute-start) | collective-permute-done | bytes 524320 | tf_op jit(solution)/shard_map/while/body/eval_jaxpr/ppermute | solution.py:17
  105.1 7.2 %collective-permute-done = bf16[2,16,64,128]{3,2,1,0:T(8,128)(2,1)} collective-permute-done((bf16[2,16,64,128]{3,2,1,0:T(8,128)(2,1)}, bf16[2,16,64,128]{3,2,1,0:T(8,128)(2,1)}, u32[]{:S(2)}, u32[]{:S(2)}) %collective-permute-start) | collective-permute-done | bytes 524320 | tf_op jit(solution)/shard_map/while/body/eval_jaxpr/ppermute | solution.py:17
  121.9 6.4 %collective-permute-done = bf16[2,16,64,128]{3,2,1,0:T(8,128)(2,1)} collective-permute-done((bf16[2,16,64,128]{3,2,1,0:T(8,128)(2,1)}, bf16[2,16,64,128]{3,2,1,0:T(8,128)(2,1)}, u32[]{:S(2)}, u32[]{:S(2)}) %collective-permute-start) | collective-permute-done | bytes 524320 | tf_op jit(solution)/shard_map/while/body/eval_jaxpr/ppermute | solution.py:17
  137.9 6.4 %collective-permute-done = bf16[2,16,64,128]{3,2,1,0:T(8,128)(2,1)} collective-permute-done((bf16[2,16,64,128]{3,2,1,0:T(8,128)(2,1)}, bf16[2,16,64,128]{3,2,1,0:T(8,128)(2,1)}, u32[]{:S(2)}, u32[]{:S(2)}) %collective-permute-start) | collective-permute-done | bytes 524320 | tf_op jit(solution)/shard_map/while/body/eval_jaxpr/ppermute | solution.py:17
  153.9 6.4 %collective-permute-done = bf16[2,16,64,128]{3,2,1,0:T(8,128)(2,1)} collective-permute-done((bf16[2,16,64,128]{3,2,1,0:T(8,128)(2,1)}, bf16[2,16,64,128]{3,2,1,0:T(8,128)(2,1)}, u32[]{:S(2)}, u32[]{:S(2)}) %collective-permute-start) | collective-permute-done | bytes 524320 | tf_op jit(solution)/shard_map/while/body/eval_jaxpr/ppermute | solution.py:17
  169.7 6.4 %collective-permute-done = bf16[2,16,64,128]{3,2,1,0:T(8,128)(2,1)} collective-permute-done((bf16[2,16,64,128]{3,2,1,0:T(8,128)(2,1)}, bf16[2,16,64,128]{3,2,1,0:T(8,128)(2,1)}, u32[]{:S(2)}, u32[]{:S(2)}) %collective-permute-start) | collective-permute-done | bytes 524320 | tf_op jit(solution)/shard_map/while/body/eval_jaxpr/ppermute | solution.py:17
  185.4 6.4 %collective-permute-done = bf16[2,16,64,128]{3,2,1,0:T(8,128)(2,1)} collective-permute-done((bf16[2,16,64,128]{3,2,1,0:T(8,128)(2,1)}, bf16[2,16,64,128]{3,2,1,0:T(8,128)(2,1)}, u32[]{:S(2)}, u32[]{:S(2)}) %collective-permute-start) | collective-permute-done | bytes 524320 | tf_op jit(solution)/shard_map/while/body/eval_jaxpr/ppermute | solution.py:17
  201.1 6.4 %collective-permute-done = bf16[2,16,64,128]{3,2,1,0:T(8,128)(2,1)} collective-permute-done((bf16[2,16,64,128]{3,2,1,0:T(8,128)(2,1)}, bf16[2,16,64,128]{3,2,1,0:T(8,128)(2,1)}, u32[]{:S(2)}, u32[]{:S(2)}) %collective-permute-start) | collective-permute-done | bytes 524320 | tf_op jit(solution)/shard_map/while/body/eval_jaxpr/ppermute | solution.py:17
  216.8 7.2 %collective-permute-done = bf16[2,16,64,128]{3,2,1,0:T(8,128)(2,1)} collective-permute-done((bf16[2,16,64,128]{3,2,1,0:T(8,128)(2,1)}, bf16[2,16,64,128]{3,2,1,0:T(8,128)(2,1)}, u32[]{:S(2)}, u32[]{:S(2)}) %collective-permute-start) | collective-permute-done | bytes 524320 | tf_op jit(solution)/shard_map/while/body/eval_jaxpr/ppermute | solution.py:17
  227.4 6.4 %collective-permute-start = (bf16[2,16,64,128]{3,2,1,0:T(8,128)(2,1)}, bf16[2,16,64,128]{3,2,1,0:T(8,128)(2,1)}, u32[]{:S(2)}, u32[]{:S(2)}) collective-permute-start(bf16[2,16,64,128]{3,2,1,0:T(8,128)(2,1)} %fusion.47), channel_id=1, source_target_pairs={{0,16},{16,32},{32,48},{48,64},{64,80},{80,96},{96,112},{112,128},... | collective-permute-start | bytes 1572872 | tf_op jit(solution)/shard_map/while/body/eval_jaxpr/ppermute | solution.py:17
  233.8 8.3 %collective-permute-done = bf16[2,16,64,128]{3,2,1,0:T(8,128)(2,1)} collective-permute-done((bf16[2,16,64,128]{3,2,1,0:T(8,128)(2,1)}, bf16[2,16,64,128]{3,2,1,0:T(8,128)(2,1)}, u32[]{:S(2)}, u32[]{:S(2)}) %collective-permute-start) | collective-permute-done | bytes 524320 | tf_op jit(solution)/shard_map/while/body/eval_jaxpr/ppermute | solution.py:17
  245.5 6.5 %collective-permute-start = (bf16[2,16,64,128]{3,2,1,0:T(8,128)(2,1)}, bf16[2,16,64,128]{3,2,1,0:T(8,128)(2,1)}, u32[]{:S(2)}, u32[]{:S(2)}) collective-permute-start(bf16[2,16,64,128]{3,2,1,0:T(8,128)(2,1)} %fusion.47), channel_id=1, source_target_pairs={{0,16},{16,32},{32,48},{48,64},{64,80},{80,96},{96,112},{112,128},... | collective-permute-start | bytes 1572872 | tf_op jit(solution)/shard_map/while/body/eval_jaxpr/ppermute | solution.py:17
  252.0 9.5 %collective-permute-done = bf16[2,16,64,128]{3,2,1,0:T(8,128)(2,1)} collective-permute-done((bf16[2,16,64,128]{3,2,1,0:T(8,128)(2,1)}, bf16[2,16,64,128]{3,2,1,0:T(8,128)(2,1)}, u32[]{:S(2)}, u32[]{:S(2)}) %collective-permute-start) | collective-permute-done | bytes 524320 | tf_op jit(solution)/shard_map/while/body/eval_jaxpr/ppermute | solution.py:17
  264.8 6.5 %collective-permute-start = (bf16[2,16,64,128]{3,2,1,0:T(8,128)(2,1)}, bf16[2,16,64,128]{3,2,1,0:T(8,128)(2,1)}, u32[]{:S(2)}, u32[]{:S(2)}) collective-permute-start(bf16[2,16,64,128]{3,2,1,0:T(8,128)(2,1)} %fusion.47), channel_id=1, source_target_pairs={{0,16},{16,32},{32,48},{48,64},{64,80},{80,96},{96,112},{112,128},... | collective-permute-start | bytes 1572872 | tf_op jit(solution)/shard_map/while/body/eval_jaxpr/ppermute | solution.py:17
  271.4 10.6 %collective-permute-done = bf16[2,16,64,128]{3,2,1,0:T(8,128)(2,1)} collective-permute-done((bf16[2,16,64,128]{3,2,1,0:T(8,128)(2,1)}, bf16[2,16,64,128]{3,2,1,0:T(8,128)(2,1)}, u32[]{:S(2)}, u32[]{:S(2)}) %collective-permute-start) | collective-permute-done | bytes 524320 | tf_op jit(solution)/shard_map/while/body/eval_jaxpr/ppermute | solution.py:17
  285.1 8.8 %fusion.16 = f32[2,256,16,64]{1,3,2,0:T(8,128)} fusion(bf16[2,256,16,64]{1,3,2,0:T(8,128)(2,1)S(1)} %bitcast.65, f32[2,16,64,256]{3,2,1,0:T(8,128)S(1)} %fusion.32, f32[2,16,64,256]{3,2,1,0:T(8,128)S(1)} %copy-done.3, f32[2,16,256]{2,1,0:T(8,128)S(1)} %copy-done.11, f32[2,256,256]{2,1,0:T(8,128)} %fusion.39, f32[256,256]{1,0:T(8,128)S(1)} %copy-done.6, ...), kind=kOutput, calls=%fused_computation.22 | convolution fusion | flops 1624768512 | bytes 8224896 | tf_op jit(solution)/shard_map/while/body/eval_jaxpr/mhij,mjhp->mihp/dot_general | solution.py:60
  299.2 39.0 %psum.7 = f32[2,256]{1,0:T(2,128)S(1)} all-reduce(f32[2,256]{1,0:T(2,128)S(1)} %multiply_reduce_fusion), channel_id=1, replica_groups=mesh['seq'=16,'head'=16] {'head'}, use_global_device_ids=true, to_apply=%region_5.6 | all-reduce | flops 512 | bytes 4096 | tf_op jit(solution)/shard_map/psum | solution.py:113
  341.7 126.2 %all-gather.2.cloned.1.call-done = bf16[2,4096,1024]{2,1,0:T(8,128)(2,1)} async-done(((bf16[2,256,1024]{2,1,0:T(8,128)(2,1)}), bf16[2,4096,1024]{2,1,0:T(8,128)(2,1)}) %all-gather.2.cloned.1.call-update) | async-done | bytes 16777232 | tf_op jit(solution)/shard_map/all_gather | solution.py:120
  467.9 16.9 %convolution_convert_fusion = bf16[2,4096,512]{2,1,0:T(8,128)(2,1)} fusion(bf16[2,4096,1024]{2,1,0:T(8,128)(2,1)} %all-gather.2.cloned.1.call-done, bf16[2,1024,512]{2,1,0:T(8,128)(2,1)S(1)} %copy-done), kind=kOutput, calls=%fused_computation.10 | convolution fusion | flops 8594128896 | bytes 27262976 | tf_op jit(solution)/shard_map/mtk,mkd->mtd/dot_general | solution.py:118
  484.8 66.5 %reduce-scatter.2.cloned.1.call-done = bf16[2,256,512]{2,1,0:T(8,128)(2,1)} async-done(((bf16[2,4096,512]{2,1,0:T(8,128)(2,1)}), bf16[2,256,512]{2,1,0:T(8,128)(2,1)}) %reduce-scatter.2.cloned.1.call-update) | async-done | bytes 524304 | tf_op jit(solution)/shard_map/reduce_scatter | solution.py:124
  (106 shorter events, 144.1 us)
Async XLA Ops:
  6.5 461.4 %copy-start = (bf16[2,1024,512]{2,1,0:T(8,128)(2,1)S(1)}, bf16[2,1024,512]{2,1,0:T(8,128)(2,1)}, u32[]{:S(2)}) copy-start(bf16[2,1024,512]{2,1,0:T(8,128)(2,1)} %param.22) | copy-start | bytes 6291460
  6.5 13.3 %copy-start.4 = (bf16[2,256,128]{2,1,0:T(8,128)(2,1)S(1)}, bf16[2,256,128]{2,1,0:T(8,128)(2,1)}, u32[]{:S(2)}) copy-start(bf16[2,256,128]{2,1,0:T(8,128)(2,1)} %param.16) | copy-start | bytes 393220
  6.5 13.3 %copy-start.5 = (bf16[2,256,128]{2,1,0:T(8,128)(2,1)S(1)}, bf16[2,256,128]{2,1,0:T(8,128)(2,1)}, u32[]{:S(2)}) copy-start(bf16[2,256,128]{2,1,0:T(8,128)(2,1)} %param.15) | copy-start | bytes 393220
  6.5 461.4 %all-gather.2.cloned.1.call-start = ((), (), s32[]{:S(2)}) async-start(), calls=%async_computation.1 | async-start | bytes 17825792 | tf_op jit(solution)/shard_map/all_gather | solution.py:120
  8.0 15.1 %collective-permute-start.1 = (s32[1]{0:T(128)}, s32[1]{0:T(128)}, u32[]{:S(2)}, u32[]{:S(2)}) collective-permute-start(s32[1]{0:T(128)} %slice.25), channel_id=1, source_target_pairs={{0,16},{16,32},{32,48},{48,64},{64,80},{80,96},{96,112},{112,128},... | collective-permute-start | bytes 20 | tf_op jit(solution)/shard_map/ppermute | solution.py:17
  16.6 9.2 %copy-start.14 = (f32[2,16]{1,0:T(2,128)S(1)}, f32[2,16]{1,0:T(2,128)}, u32[]{:S(2)}) copy-start(f32[2,16]{1,0:T(2,128)} %param.18) | copy-start | bytes 388
  30.6 253.6 %copy-start.6 = (f32[256,256]{1,0:T(8,128)S(1)}, f32[256,256]{1,0:T(8,128)}, u32[]{:S(2)}) copy-start(f32[256,256]{1,0:T(8,128)} %fusion.30) | copy-start | bytes 786436
  32.9 14.7 %collective-permute-start = (bf16[2,16,64,128]{3,2,1,0:T(8,128)(2,1)}, bf16[2,16,64,128]{3,2,1,0:T(8,128)(2,1)}, u32[]{:S(2)}, u32[]{:S(2)}) collective-permute-start(bf16[2,16,64,128]{3,2,1,0:T(8,128)(2,1)} %fusion.47), channel_id=1, source_target_pairs={{0,16},{16,32},{32,48},{48,64},{64,80},{80,96},{96,112},{112,128},... | collective-permute-start | bytes 1572872 | tf_op jit(solution)/shard_map/while/body/eval_jaxpr/ppermute | solution.py:17
  51.0 13.9 %collective-permute-start = (bf16[2,16,64,128]{3,2,1,0:T(8,128)(2,1)}, bf16[2,16,64,128]{3,2,1,0:T(8,128)(2,1)}, u32[]{:S(2)}, u32[]{:S(2)}) collective-permute-start(bf16[2,16,64,128]{3,2,1,0:T(8,128)(2,1)} %fusion.47), channel_id=1, source_target_pairs={{0,16},{16,32},{32,48},{48,64},{64,80},{80,96},{96,112},{112,128},... | collective-permute-start | bytes 1572872 | tf_op jit(solution)/shard_map/while/body/eval_jaxpr/ppermute | solution.py:17
  68.2 13.0 %collective-permute-start = (bf16[2,16,64,128]{3,2,1,0:T(8,128)(2,1)}, bf16[2,16,64,128]{3,2,1,0:T(8,128)(2,1)}, u32[]{:S(2)}, u32[]{:S(2)}) collective-permute-start(bf16[2,16,64,128]{3,2,1,0:T(8,128)(2,1)} %fusion.47), channel_id=1, source_target_pairs={{0,16},{16,32},{32,48},{48,64},{64,80},{80,96},{96,112},{112,128},... | collective-permute-start | bytes 1572872 | tf_op jit(solution)/shard_map/while/body/eval_jaxpr/ppermute | solution.py:17
  84.6 12.1 %collective-permute-start = (bf16[2,16,64,128]{3,2,1,0:T(8,128)(2,1)}, bf16[2,16,64,128]{3,2,1,0:T(8,128)(2,1)}, u32[]{:S(2)}, u32[]{:S(2)}) collective-permute-start(bf16[2,16,64,128]{3,2,1,0:T(8,128)(2,1)} %fusion.47), channel_id=1, source_target_pairs={{0,16},{16,32},{32,48},{48,64},{64,80},{80,96},{96,112},{112,128},... | collective-permute-start | bytes 1572872 | tf_op jit(solution)/shard_map/while/body/eval_jaxpr/ppermute | solution.py:17
  100.2 12.1 %collective-permute-start = (bf16[2,16,64,128]{3,2,1,0:T(8,128)(2,1)}, bf16[2,16,64,128]{3,2,1,0:T(8,128)(2,1)}, u32[]{:S(2)}, u32[]{:S(2)}) collective-permute-start(bf16[2,16,64,128]{3,2,1,0:T(8,128)(2,1)} %fusion.47), channel_id=1, source_target_pairs={{0,16},{16,32},{32,48},{48,64},{64,80},{80,96},{96,112},{112,128},... | collective-permute-start | bytes 1572872 | tf_op jit(solution)/shard_map/while/body/eval_jaxpr/ppermute | solution.py:17
  115.7 12.6 %collective-permute-start = (bf16[2,16,64,128]{3,2,1,0:T(8,128)(2,1)}, bf16[2,16,64,128]{3,2,1,0:T(8,128)(2,1)}, u32[]{:S(2)}, u32[]{:S(2)}) collective-permute-start(bf16[2,16,64,128]{3,2,1,0:T(8,128)(2,1)} %fusion.47), channel_id=1, source_target_pairs={{0,16},{16,32},{32,48},{48,64},{64,80},{80,96},{96,112},{112,128},... | collective-permute-start | bytes 1572872 | tf_op jit(solution)/shard_map/while/body/eval_jaxpr/ppermute | solution.py:17
  131.7 12.6 %collective-permute-start = (bf16[2,16,64,128]{3,2,1,0:T(8,128)(2,1)}, bf16[2,16,64,128]{3,2,1,0:T(8,128)(2,1)}, u32[]{:S(2)}, u32[]{:S(2)}) collective-permute-start(bf16[2,16,64,128]{3,2,1,0:T(8,128)(2,1)} %fusion.47), channel_id=1, source_target_pairs={{0,16},{16,32},{32,48},{48,64},{64,80},{80,96},{96,112},{112,128},... | collective-permute-start | bytes 1572872 | tf_op jit(solution)/shard_map/while/body/eval_jaxpr/ppermute | solution.py:17
  147.7 12.6 %collective-permute-start = (bf16[2,16,64,128]{3,2,1,0:T(8,128)(2,1)}, bf16[2,16,64,128]{3,2,1,0:T(8,128)(2,1)}, u32[]{:S(2)}, u32[]{:S(2)}) collective-permute-start(bf16[2,16,64,128]{3,2,1,0:T(8,128)(2,1)} %fusion.47), channel_id=1, source_target_pairs={{0,16},{16,32},{32,48},{48,64},{64,80},{80,96},{96,112},{112,128},... | collective-permute-start | bytes 1572872 | tf_op jit(solution)/shard_map/while/body/eval_jaxpr/ppermute | solution.py:17
  163.7 12.3 %collective-permute-start = (bf16[2,16,64,128]{3,2,1,0:T(8,128)(2,1)}, bf16[2,16,64,128]{3,2,1,0:T(8,128)(2,1)}, u32[]{:S(2)}, u32[]{:S(2)}) collective-permute-start(bf16[2,16,64,128]{3,2,1,0:T(8,128)(2,1)} %fusion.47), channel_id=1, source_target_pairs={{0,16},{16,32},{32,48},{48,64},{64,80},{80,96},{96,112},{112,128},... | collective-permute-start | bytes 1572872 | tf_op jit(solution)/shard_map/while/body/eval_jaxpr/ppermute | solution.py:17
  179.5 12.3 %collective-permute-start = (bf16[2,16,64,128]{3,2,1,0:T(8,128)(2,1)}, bf16[2,16,64,128]{3,2,1,0:T(8,128)(2,1)}, u32[]{:S(2)}, u32[]{:S(2)}) collective-permute-start(bf16[2,16,64,128]{3,2,1,0:T(8,128)(2,1)} %fusion.47), channel_id=1, source_target_pairs={{0,16},{16,32},{32,48},{48,64},{64,80},{80,96},{96,112},{112,128},... | collective-permute-start | bytes 1572872 | tf_op jit(solution)/shard_map/while/body/eval_jaxpr/ppermute | solution.py:17
  195.2 12.3 %collective-permute-start = (bf16[2,16,64,128]{3,2,1,0:T(8,128)(2,1)}, bf16[2,16,64,128]{3,2,1,0:T(8,128)(2,1)}, u32[]{:S(2)}, u32[]{:S(2)}) collective-permute-start(bf16[2,16,64,128]{3,2,1,0:T(8,128)(2,1)} %fusion.47), channel_id=1, source_target_pairs={{0,16},{16,32},{32,48},{48,64},{64,80},{80,96},{96,112},{112,128},... | collective-permute-start | bytes 1572872 | tf_op jit(solution)/shard_map/while/body/eval_jaxpr/ppermute | solution.py:17
  210.9 13.1 %collective-permute-start = (bf16[2,16,64,128]{3,2,1,0:T(8,128)(2,1)}, bf16[2,16,64,128]{3,2,1,0:T(8,128)(2,1)}, u32[]{:S(2)}, u32[]{:S(2)}) collective-permute-start(bf16[2,16,64,128]{3,2,1,0:T(8,128)(2,1)} %fusion.47), channel_id=1, source_target_pairs={{0,16},{16,32},{32,48},{48,64},{64,80},{80,96},{96,112},{112,128},... | collective-permute-start | bytes 1572872 | tf_op jit(solution)/shard_map/while/body/eval_jaxpr/ppermute | solution.py:17
  227.4 14.7 %collective-permute-start = (bf16[2,16,64,128]{3,2,1,0:T(8,128)(2,1)}, bf16[2,16,64,128]{3,2,1,0:T(8,128)(2,1)}, u32[]{:S(2)}, u32[]{:S(2)}) collective-permute-start(bf16[2,16,64,128]{3,2,1,0:T(8,128)(2,1)} %fusion.47), channel_id=1, source_target_pairs={{0,16},{16,32},{32,48},{48,64},{64,80},{80,96},{96,112},{112,128},... | collective-permute-start | bytes 1572872 | tf_op jit(solution)/shard_map/while/body/eval_jaxpr/ppermute | solution.py:17
  245.5 16.0 %collective-permute-start = (bf16[2,16,64,128]{3,2,1,0:T(8,128)(2,1)}, bf16[2,16,64,128]{3,2,1,0:T(8,128)(2,1)}, u32[]{:S(2)}, u32[]{:S(2)}) collective-permute-start(bf16[2,16,64,128]{3,2,1,0:T(8,128)(2,1)} %fusion.47), channel_id=1, source_target_pairs={{0,16},{16,32},{32,48},{48,64},{64,80},{80,96},{96,112},{112,128},... | collective-permute-start | bytes 1572872 | tf_op jit(solution)/shard_map/while/body/eval_jaxpr/ppermute | solution.py:17
  264.8 17.1 %collective-permute-start = (bf16[2,16,64,128]{3,2,1,0:T(8,128)(2,1)}, bf16[2,16,64,128]{3,2,1,0:T(8,128)(2,1)}, u32[]{:S(2)}, u32[]{:S(2)}) collective-permute-start(bf16[2,16,64,128]{3,2,1,0:T(8,128)(2,1)} %fusion.47), channel_id=1, source_target_pairs={{0,16},{16,32},{32,48},{48,64},{64,80},{80,96},{96,112},{112,128},... | collective-permute-start | bytes 1572872 | tf_op jit(solution)/shard_map/while/body/eval_jaxpr/ppermute | solution.py:17
  296.9 41.3 %copy-start.13 = (f32[2,1024]{1,0:T(2,128)S(1)}, f32[2,1024]{1,0:T(2,128)}, u32[]{:S(2)}) copy-start(f32[2,1024]{1,0:T(2,128)} %param.21) | copy-start | bytes 24580
  341.5 209.8 %reduce-scatter.2.cloned.1.call-start = ((), (), s32[]{:S(2)}) async-start(), calls=%async_computation.2 | async-start | bytes 8912896 | tf_op jit(solution)/shard_map/reduce_scatter | solution.py:124
  (10 other events, 30.1 us)
Sparse Core Ops, SparseCore 0:
  341.6 126.2 all-gather.1
  484.9 66.3 reduce-scatter.1
where the time goes:
time: 565 us; the launch traced here: 558 us
  waiting for transfers between devices  316 us (56%)
  starting transfers between devices  81.6 us (14%)
  other arithmetic  63.8 us (11%)
  blocking collectives  39 us (7%)
  matrix products  34.3 us (6%)
  between operations  13.5 us (2%)
  local copies, waits for them, and re-layouts  9.44 us (2%)
    all_gather x1, waiting for transfers between devices, local(): lax.all_gather(normed, 'seq', axis=1, tiled=True)  126 us
    ppermute x16, waiting for transfers between devices, passed_along(): return lax.ppermute(block, axis, route)  123 us
    ppermute x16, starting transfers between devices, passed_along(): return lax.ppermute(block, axis, route)  81.4 us
    reduce_scatter x1, waiting for transfers between devices, local(): lax.psum_scatter(partial_terms.astype(jnp.bfloat16), 'head', scatter_dime...  66.5 us
    psum x1, blocking collectives, local(): square_sum = lax.psum(jnp.sum(gated * gated, axis=2), 'head')  39 us
    convert_element_type x15, other arithmetic, relay_turn(): outgoing.astype(jnp.bfloat16)  33.3 us
    convert_element_type x15, other arithmetic, relay_turn(): passed_along(outgoing.astype(jnp.bfloat16), 'seq', 1).astype(outgoing.dtype)  17.2 us
    dot_general x1, matrix products, local(): jnp.einsum('mtk,mkd->mtd', lax.all_gather(normed, 'seq', axis=1, tiled=Tr...  16.9 us
  transfers between devices with their start and end apart: 18, of which 17 were waited for; matrix products, arithmetic and copies ran while one was open for 2% of the time, Pallas kernels for 0%

commit v1 on v0

--- a/solution.py
+++ b/solution.py
@@ -98,11 +98,13 @@
     factor_all = from_blocks(factors)
     decay_dev = factor_all[:, -1, :]
 
-    def relay_turn(counter, incoming):
-        outgoing = local_state + decay_dev[:, :, None, None] * incoming
-        return passed_along(outgoing.astype(jnp.bfloat16), "seq", 1).astype(outgoing.dtype)
-
-    state_in = lax.fori_loop(0, lax.axis_size("seq") - 1, relay_turn, jnp.zeros_like(local_state))
+    decay_one = passed_along(decay_dev, "seq", 1)
+    decay_two = passed_along(decay_dev, "seq", 2)
+    earlier = passed_along(local_state.astype(jnp.bfloat16), "seq", 1).astype(jnp.float32)
+    pair_state = (local_state + decay_dev[:, :, None, None] * earlier).astype(jnp.bfloat16)
+    near = passed_along(pair_state, "seq", 1).astype(jnp.float32)
+    far = passed_along(pair_state, "seq", 3).astype(jnp.float32)
+    state_in = near + (decay_one * decay_two)[:, :, None, None] * far
     entering = jnp.einsum("mtn,mhpn->mthp", c_float, state_in, precision=highest)
     ssd_out = (
         from_blocks(outputs) + factor_all[..., None] * entering + skip_d[:, None, :, None] * x_float

time: 565 us -> 310 us (0.55)
  waiting for transfers between devices: 316 us -> 200 us
  starting transfers between devices: 81.6 us -> 20 us
  other arithmetic: 63.8 us -> 10.8 us
  blocking collectives: 39 us -> 25.5 us
  matrix products: 34.3 us -> 28.5 us
    ppermute x16 -> x6, waiting for transfers between devices: 123 us -> 8.6 us  [passed_along(): return lax.ppermute(block, axis, route)]
    ppermute x16 -> x6, starting transfers between devices: 81.4 us -> 19.7 us  [passed_along(): return lax.ppermute(block, axis, route)]
    convert_element_type x31 -> x2, other arithmetic: 51.8 us -> 1.49 us  [the longest x1 1.28 us: span_state(): kept = (seg_block == before).astype(jnp.float32)]
    psum x1, blocking collectives: 39 us -> 25.5 us  [local(): square_sum = lax.psum(jnp.sum(gated * gated, axis=2), 'head')]
  transfers between devices with their start and end apart: 18 -> 8, of which waited for: 17 -> 5; matrix products, arithmetic and copies ran while one was open for 2% -> 4% of each run, Pallas kernels for 0% -> 0%
where the time goes in v1:
time: 310 us; the launch traced here: 305 us
  waiting for transfers between devices  200 us (65%)
  matrix products  28.5 us (9%)
  blocking collectives  25.5 us (8%)
  starting transfers between devices  20 us (6%)
  between operations  13.6 us (4%)
  other arithmetic  10.8 us (3%)
  local copies, waits for them, and re-layouts  7.02 us (2%)
    all_gather x1, waiting for transfers between devices, local(): lax.all_gather(normed, 'seq', axis=1, tiled=True)  125 us
    reduce_scatter x1, waiting for transfers between devices, local(): lax.psum_scatter(partial_terms.astype(jnp.bfloat16), 'head', scatter_dime...  66.5 us
    psum x1, blocking collectives, local(): square_sum = lax.psum(jnp.sum(gated * gated, axis=2), 'head')  25.5 us
    ppermute x6, starting transfers between devices, passed_along(): return lax.ppermute(block, axis, route)  19.7 us
    dot_general x1, matrix products, local(): jnp.einsum('mtk,mkd->mtd', lax.all_gather(normed, 'seq', axis=1, tiled=Tr...  16.9 us
    ppermute x6, waiting for transfers between devices, passed_along(): return lax.ppermute(block, axis, route)  8.6 us
    dot_general x1, matrix products, span_output(): inside = jnp.einsum('mhij,mjhp->mihp', weights, x_block, precision=highest)  6.36 us
  transfers between devices with their start and end apart: 8, of which 5 were waited for; matrix products, arithmetic and copies ran while one was open for 4% of the time, Pallas kernels for 0%

profile of v1, /device:TPU:41, one launch (start us, length us, event | category | flops | bytes accessed | tf_op | source)
XLA Modules:
  0.0 305.1 jit_solution(1519707325484328579)
XLA Ops:
  6.6 1.4 slice.25
  8.0 3.2 %collective-permute-start = (s32[1]{0:T(128)}, s32[1]{0:T(128)}, u32[]{:S(2)}, u32[]{:S(2)}) collective-permute-start(s32[1]{0:T(128)} %slice.25), channel_id=1, source_target_pairs={{0,16},{16,32},{32,48},{48,64},{64,80},{80,96},{96,112},{112,128},... | collective-permute-start | bytes 20 | tf_op jit(solution)/shard_map/ppermute | solution.py:17
  12.8 1.2 reduce-window.6
  14.4 1.5 copy.17
  16.1 1.3 compare_convert_fusion.1
  18.8 1.2 fusion.39
  20.0 2.9 collective-permute-start.1
  23.0 1.0 fusion.28
  24.2 3.8 %collective-permute-start.4 = (f32[2,16]{1,0:T(2,128)S(1)}, f32[2,16]{1,0:T(2,128)S(1)}, u32[]{:S(2)}, u32[]{:S(2)}) collective-permute-start(f32[2,16]{1,0:T(2,128)S(1)} %slice_reduce_fusion.1), channel_id=1, source_target_pairs={{0,32},{16,48},{32,64},{48,80},{64,96},{80,112},{96,128},{112,144}... | collective-permute-start | bytes 392 | tf_op jit(solution)/shard_map/ppermute | solution.py:17
  28.0 2.6 collective-permute-start.3
  30.6 3.9 %collective-permute-done.1 = bf16[2,16,64,128]{3,2,1,0:T(8,128)(2,1)S(1)} collective-permute-done((bf16[2,16,64,128]{3,2,1,0:T(8,128)(2,1)S(1)}, bf16[2,16,64,128]{3,2,1,0:T(8,128)(2,1)S(1)}, u32[]{:S(2)}, u32[]{:S(2)}) %collective-permute-start.1) | collective-permute-done | bytes 524320 | tf_op jit(solution)/shard_map/ppermute | solution.py:17
  34.6 5.1 %collective-permute-start.5 = (bf16[2,16,64,128]{3,2,1,0:T(8,128)(2,1)S(1)}, bf16[2,16,64,128]{3,2,1,0:T(8,128)(2,1)S(1)}, u32[]{:S(2)}, u32[]{:S(2)}) collective-permute-start(bf16[2,16,64,128]{3,2,1,0:T(8,128)(2,1)S(1)} %add_convert_fusion), channel_id=1, source_target_pairs={{0,48},{16,64},{32,80},{48,96},{64,112},{80,128},{96,144},{112,160... | collective-permute-start | bytes 1572872 | tf_op jit(solution)/shard_map/ppermute | solution.py:17
  39.8 2.1 collective-permute-start.2
  41.9 6.4 %fusion = f32[2,16,256,64]{2,3,1,0:T(8,128)S(1)} fusion(bf16[2,256,16,64]{1,3,2,0:T(8,128)(2,1)S(1)} %bitcast.63, f32[2,16,256]{2,1,0:T(8,128)S(1)} %get-tuple-element.30, f32[2,256,256]{2,1,0:T(8,128)S(1)} %fusion.40, f32[256,256]{1,0:T(8,128)S(1)} %fusion.31, f32[2,16,256]{2,1,0:T(8,128)S(1)} %get-tuple-element.33), kind=kOutput, calls=%fused_computation | convolution fusion | flops 1621098496 | bytes 3997696 | tf_op jit(solution)/shard_map/while/body/eval_jaxpr/mhij,mjhp->mihp/dot_general | solution.py:60
  48.3 0.9 collective-permute-done.5
  49.2 3.9 %collective-permute-done.2 = bf16[2,16,64,128]{3,2,1,0:T(8,128)(2,1)S(1)} collective-permute-done((bf16[2,16,64,128]{3,2,1,0:T(8,128)(2,1)S(1)}, bf16[2,16,64,128]{3,2,1,0:T(8,128)(2,1)S(1)}, u32[]{:S(2)}, u32[]{:S(2)}) %collective-permute-start.2) | collective-permute-done | bytes 524320 | tf_op jit(solution)/shard_map/ppermute | solution.py:17
  53.0 2.9 fusion.14
  55.9 3.0 copy.18
  58.9 2.3 multiply_reduce_fusion
  61.2 25.5 %psum.7 = f32[2,256]{1,0:T(2,128)S(1)} all-reduce(f32[2,256]{1,0:T(2,128)S(1)} %multiply_reduce_fusion), channel_id=1, replica_groups=mesh['seq'=16,'head'=16] {'head'}, use_global_device_ids=true, to_apply=%region_3.4 | all-reduce | flops 512 | bytes 4096 | tf_op jit(solution)/shard_map/psum | solution.py:115
  86.8 3.3 %multiply_convert_fusion = bf16[2,256,1024]{2,1,0:T(8,128)(2,1)} fusion(f32[2,1024]{1,0:T(2,128)S(1)} %copy-done.6, f32[2,256]{1,0:T(2,128)S(1)} %add_rsqrt_fusion, f32[2,256,1024]{2,1,0:T(8,128)} %copy.18, bf16[2,256,1024]{2,1,0:T(8,128)(2,1)S(1)} %copy-done.1), kind=kLoop, calls=%fused_computation.28 | loop fusion | flops 4718592 | bytes 4204544 | tf_op jit(solution)/shard_map/convert_element_type | solution.py:117
  90.4 124.5 %all-gather.2.cloned.1.call-done = bf16[2,4096,1024]{2,1,0:T(8,128)(2,1)} async-done(((bf16[2,256,1024]{2,1,0:T(8,128)(2,1)}), bf16[2,4096,1024]{2,1,0:T(8,128)(2,1)}) %all-gather.2.cloned.1.call-update) | async-done | bytes 16777232 | tf_op jit(solution)/shard_map/all_gather | solution.py:122
  214.9 16.9 %convolution_convert_fusion = bf16[2,4096,512]{2,1,0:T(8,128)(2,1)} fusion(bf16[2,4096,1024]{2,1,0:T(8,128)(2,1)} %all-gather.2.cloned.1.call-done, bf16[2,1024,512]{2,1,0:T(8,128)(2,1)S(1)} %copy-done), kind=kOutput, calls=%fused_computation.7 | convolution fusion | flops 8594128896 | bytes 27262976 | tf_op jit(solution)/shard_map/mtk,mkd->mtd/dot_general | solution.py:120
  231.8 66.5 %reduce-scatter.2.cloned.1.call-done = bf16[2,256,512]{2,1,0:T(8,128)(2,1)} async-done(((bf16[2,4096,512]{2,1,0:T(8,128)(2,1)}), bf16[2,256,512]{2,1,0:T(8,128)(2,1)}) %reduce-scatter.2.cloned.1.call-update) | async-done | bytes 524304 | tf_op jit(solution)/shard_map/reduce_scatter | solution.py:126
  (41 shorter events, 4.4 us)
Async XLA Ops:
  6.5 208.4 %copy-start = (bf16[2,1024,512]{2,1,0:T(8,128)(2,1)S(1)}, bf16[2,1024,512]{2,1,0:T(8,128)(2,1)}, u32[]{:S(2)}) copy-start(bf16[2,1024,512]{2,1,0:T(8,128)(2,1)} %param.20) | copy-start | bytes 6291460
  6.5 9.6 %copy-start.5 = (s32[256]{0:T(256)S(1)}, s32[256]{0:T(256)}, u32[]{:S(2)}) copy-start(s32[256]{0:T(256)} %param.21) | copy-start | bytes 3076
  6.5 12.1 %copy-start.7 = (f32[2,16]{1,0:T(2,128)S(1)}, f32[2,16]{1,0:T(2,128)}, u32[]{:S(2)}) copy-start(f32[2,16]{1,0:T(2,128)} %param.16) | copy-start | bytes 388
  6.5 12.1 %copy-start.4 = (f32[2,256,16]{1,2,0:T(8,128)S(1)}, f32[2,256,16]{1,2,0:T(8,128)}, u32[]{:S(2)}) copy-start(f32[2,256,16]{1,2,0:T(8,128)} %param.15) | copy-start | bytes 98308
  6.5 9.3 %copy-start.2 = (bf16[2,256,128]{2,1,0:T(8,128)(2,1)S(1)}, bf16[2,256,128]{2,1,0:T(8,128)(2,1)}, u32[]{:S(2)}) copy-start(bf16[2,256,128]{2,1,0:T(8,128)(2,1)} %param.14) | copy-start | bytes 393220
  6.5 9.3 %copy-start.3 = (bf16[2,256,128]{2,1,0:T(8,128)(2,1)S(1)}, bf16[2,256,128]{2,1,0:T(8,128)(2,1)}, u32[]{:S(2)}) copy-start(bf16[2,256,128]{2,1,0:T(8,128)(2,1)} %param.13) | copy-start | bytes 393220
  6.6 208.3 %all-gather.2.cloned.1.call-start = ((), (), s32[]{:S(2)}) async-start(), calls=%async_computation.1 | async-start | bytes 17825792 | tf_op jit(solution)/shard_map/all_gather | solution.py:122
  8.0 8.1 %collective-permute-start = (s32[1]{0:T(128)}, s32[1]{0:T(128)}, u32[]{:S(2)}, u32[]{:S(2)}) collective-permute-start(s32[1]{0:T(128)} %slice.25), channel_id=1, source_target_pairs={{0,16},{16,32},{32,48},{48,64},{64,80},{80,96},{96,112},{112,128},... | collective-permute-start | bytes 20 | tf_op jit(solution)/shard_map/ppermute | solution.py:17
  20.0 14.4 %collective-permute-start.1 = (bf16[2,16,64,128]{3,2,1,0:T(8,128)(2,1)S(1)}, bf16[2,16,64,128]{3,2,1,0:T(8,128)(2,1)S(1)}, u32[]{:S(2)}, u32[]{:S(2)}) collective-permute-start(bf16[2,16,64,128]{3,2,1,0:T(8,128)(2,1)S(1)} %get-tuple-element.36), channel_id=1, source_target_pairs={{0,16},{16,32},{32,48},{48,64},{64,80},{80,96},{96,112},{112,128},... | collective-permute-start | bytes 1572872 | tf_op jit(solution)/shard_map/ppermute | solution.py:17
  24.2 24.1 %collective-permute-start.4 = (f32[2,16]{1,0:T(2,128)S(1)}, f32[2,16]{1,0:T(2,128)S(1)}, u32[]{:S(2)}, u32[]{:S(2)}) collective-permute-start(f32[2,16]{1,0:T(2,128)S(1)} %slice_reduce_fusion.1), channel_id=1, source_target_pairs={{0,32},{16,48},{32,64},{48,80},{64,96},{80,112},{96,128},{112,144}... | collective-permute-start | bytes 392 | tf_op jit(solution)/shard_map/ppermute | solution.py:17
  28.0 20.3 %collective-permute-start.3 = (f32[2,16]{1,0:T(2,128)S(1)}, f32[2,16]{1,0:T(2,128)S(1)}, u32[]{:S(2)}, u32[]{:S(2)}) collective-permute-start(f32[2,16]{1,0:T(2,128)S(1)} %slice_reduce_fusion.1), channel_id=1, source_target_pairs={{0,16},{16,32},{32,48},{48,64},{64,80},{80,96},{96,112},{112,128},... | collective-permute-start | bytes 392 | tf_op jit(solution)/shard_map/ppermute | solution.py:17
  34.6 14.5 %collective-permute-start.5 = (bf16[2,16,64,128]{3,2,1,0:T(8,128)(2,1)S(1)}, bf16[2,16,64,128]{3,2,1,0:T(8,128)(2,1)S(1)}, u32[]{:S(2)}, u32[]{:S(2)}) collective-permute-start(bf16[2,16,64,128]{3,2,1,0:T(8,128)(2,1)S(1)} %add_convert_fusion), channel_id=1, source_target_pairs={{0,48},{16,64},{32,80},{48,96},{64,112},{80,128},{96,144},{112,160... | collective-permute-start | bytes 1572872 | tf_op jit(solution)/shard_map/ppermute | solution.py:17
  39.8 13.2 %collective-permute-start.2 = (bf16[2,16,64,128]{3,2,1,0:T(8,128)(2,1)S(1)}, bf16[2,16,64,128]{3,2,1,0:T(8,128)(2,1)S(1)}, u32[]{:S(2)}, u32[]{:S(2)}) collective-permute-start(bf16[2,16,64,128]{3,2,1,0:T(8,128)(2,1)S(1)} %add_convert_fusion), channel_id=1, source_target_pairs={{0,16},{16,32},{32,48},{48,64},{64,80},{80,96},{96,112},{112,128},... | collective-permute-start | bytes 1572872 | tf_op jit(solution)/shard_map/ppermute | solution.py:17
  41.9 11.1 %copy-start.8 = (f32[2,16]{1,0:T(2,128)S(1)}, f32[2,16]{1,0:T(2,128)}, u32[]{:S(2)}) copy-start(f32[2,16]{1,0:T(2,128)} %param.18) | copy-start | bytes 388
  55.9 3.0 copy-start.1
  58.9 27.9 %copy-start.6 = (f32[2,1024]{1,0:T(2,128)S(1)}, f32[2,1024]{1,0:T(2,128)}, u32[]{:S(2)}) copy-start(f32[2,1024]{1,0:T(2,128)} %param.19) | copy-start | bytes 24580
  90.1 208.2 %reduce-scatter.2.cloned.1.call-start = ((), (), s32[]{:S(2)}) async-start(), calls=%async_computation.2 | async-start | bytes 8912896 | tf_op jit(solution)/shard_map/reduce_scatter | solution.py:126
Sparse Core Ops, SparseCore 0:
  90.2 124.6 all-gather.1
  231.9 66.3 reduce-scatter.1

commit v2 on v1

--- a/solution.py
+++ b/solution.py
@@ -1,6 +1,8 @@
 import jax
 import jax.numpy as jnp
 from jax import lax
+from jax.experimental import pallas as pl
+from jax.experimental.pallas import tpu as pltpu
 from jax.sharding import PartitionSpec as P
 
 HEADS = 256
@@ -60,6 +62,389 @@
     inside = jnp.einsum("mhij,mjhp->mihp", weights, x_block, precision=highest)
     entering = jnp.einsum("min,mhpn->mihp", c_block, carried, precision=highest)
     return inside + entry_w[..., None] * entering
+
+
+MESH = pl.DeviceIdType.MESH
+XS, YS, ZS = 4, 4, 8
+
+
+class Copies:
+    def __init__(self, send, recv):
+        self.send, self.recv, self.used = send, recv, 0
+
+    def take(self, count=1):
+        first = self.used
+        self.used += count
+        return first
+
+    def remote(self, src, dst, slot, device):
+        return pltpu.make_async_remote_copy(
+            src_ref=src,
+            dst_ref=dst,
+            send_sem=self.send.at[slot],
+            recv_sem=self.recv.at[slot],
+            device_id=device,
+            device_id_type=MESH,
+        )
+
+
+def tail_kernel(n_ref, ss_ref, w_ref, out_ref, wf, nf, part, ring, fin_src, fin, sums, send, recv, local):
+    seq, head = lax.axis_index("seq"), lax.axis_index("head")
+    x, y = seq // YS, seq % YS
+    z, c = head // 2, head % 2
+    other = 1 - c
+
+    def device(x_at, y_at, z_at, c_at):
+        return {"seq": x_at * YS + y_at, "head": z_at * 2 + c_at}
+
+    copies = Copies(send, recv)
+    started = []
+
+    def start(copy):
+        copy.start()
+        started.append(copy)
+        return copy
+
+    sibling = device(x, y, z, other)
+
+    def weight_at(model):
+        return y if model == 0 else x
+
+    def weight_peer(model, step):
+        if model == 0:
+            return device(x, (y + step) % YS, z, c)
+        return device((x + step) % XS, y, z, c)
+
+    def token_at(model):
+        return x if model == 0 else y
+
+    def token_peer(model, step, core):
+        if model == 0:
+            return device((x + step) % XS, y, z, core)
+        return device(x, (y + step) % YS, z, core)
+
+    half = wf.shape[3] // 2
+    rows = nf.shape[3]
+    top, bottom = pl.ds(0, half), pl.ds(half, half)
+    weights_in = []
+    forward_later = []
+    own_local = []
+    for model in (0, 1):
+        at = weight_at(model)
+        own = pltpu.make_async_copy(w_ref.at[model], wf.at[model, at, c], local.at[model])
+        own.start()
+        own_local.append(own)
+        first = copies.take(4)
+        order = ((1, top, 0), (-1, bottom, 1), (1, bottom, 2), (-1, top, 3))
+        for step, part_rows, n in order:
+            copy = start(
+                copies.remote(
+                    w_ref.at[model, part_rows],
+                    wf.at[model, at, c, part_rows],
+                    first + n,
+                    weight_peer(model, step),
+                )
+            )
+            weights_in.append((model, step, part_rows, n, copy))
+        slot = copies.take()
+        to_sibling = start(
+            copies.remote(w_ref.at[model], wf.at[model, at, c], slot, sibling)
+        )
+        forward_later.append(to_sibling)
+
+    sums_first = copies.take(16)
+    sums_local = pltpu.make_async_copy(ss_ref, sums.at[head], local.at[2])
+    sums_sent = []
+    for i in range(16):
+        copy = pltpu.make_async_remote_copy(
+            src_ref=ss_ref,
+            dst_ref=sums.at[head],
+            send_sem=send.at[sums_first + i],
+            recv_sem=recv.at[sums_first + head],
+            device_id={"seq": (seq + i) % 16, "head": seq},
+            device_id_type=MESH,
+        )
+        sums_sent.append(copy)
+        if i == 0:
+            pl.when(head != seq)(copy.start)
+            pl.when(head == seq)(sums_local.start)
+        else:
+            copy.start()
+
+    token_in = {}
+    token_own = []
+    for model in (0, 1):
+        at = token_at(model)
+        mine = pl.ds(pl.multiple_of(c * rows, rows), rows)
+        theirs = pl.ds(pl.multiple_of(other * rows, rows), rows)
+        own = pltpu.make_async_copy(n_ref.at[model, mine], nf.at[model, c, at], local.at[3 + model])
+        own.start()
+        token_own.append(own)
+        first = copies.take(8)
+        to_sibling = start(
+            copies.remote(n_ref.at[model, theirs], nf.at[model, c, at], first + 4, sibling)
+        )
+        sends = []
+        for core in (0, 1):
+            for n, step in ((0, 1), (1, -1)):
+                piece = n_ref.at[model, pl.ds(core * rows, rows)]
+                copy = pltpu.make_async_remote_copy(
+                    src_ref=piece,
+                    dst_ref=nf.at[model, c, at],
+                    send_sem=send.at[first + 2 * core + n],
+                    recv_sem=recv.at[first + 2 * c + n],
+                    device_id=token_peer(model, step, core),
+                    device_id_type=MESH,
+                )
+                sends.append(start(copy))
+        token_in[model] = (first, to_sibling)
+
+    def arrival(dst, slot):
+        return copies.remote(dst, dst, slot, sibling)
+
+    size = YS
+    sibling_waits = []
+    opposite = []
+    for model in (0, 1):
+        at = weight_at(model)
+        for step, part_rows, n, copy in [w[1:] for w in weights_in if w[0] == model]:
+            source = (at - step + size) % size
+            copy.wait_recv()
+            if n < 2:
+                slot = copies.take()
+                onward = start(
+                    copies.remote(
+                        wf.at[model, source, c, part_rows],
+                        wf.at[model, source, c, part_rows],
+                        slot,
+                        weight_peer(model, step),
+                    )
+                )
+                opposite.append((model, step, part_rows, onward))
+            slot = copies.take()
+            sibling_waits.append(
+                start(
+                    copies.remote(
+                        wf.at[model, source, c, part_rows],
+                        wf.at[model, source, c, part_rows],
+                        slot,
+                        sibling,
+                    )
+                )
+            )
+    for model, step, part_rows, onward in opposite:
+        at = weight_at(model)
+        source = (at - 2 * step + 2 * size) % size
+        onward.wait_recv()
+        slot = copies.take()
+        sibling_waits.append(
+            start(
+                copies.remote(
+                    wf.at[model, source, c, part_rows],
+                    wf.at[model, source, c, part_rows],
+                    slot,
+                    sibling,
+                )
+            )
+        )
+
+    token_forward = {}
+    for model in (0, 1):
+        at = token_at(model)
+        first, to_sibling = token_in[model]
+        forwards = []
+        for core, n, step in ((0, 0, 1), (1, 1, -1), (1, 0, 1), (0, 1, -1)):
+            source = (at - step + size) % size
+            arrival(nf.at[model, core, source], first + 2 * core + n).wait_recv()
+            if core == n:
+                forwards.append(
+                    start(
+                        copies.remote(
+                            nf.at[model, core, source],
+                            nf.at[model, core, source],
+                            first + 5 + n,
+                            token_peer(model, step, c),
+                        )
+                    )
+                )
+        token_forward[model] = (to_sibling, forwards)
+
+    for own in own_local:
+        own.wait()
+    for copy in forward_later + sibling_waits:
+        copy.wait_recv()
+
+    def piece(model, z_to, e):
+        if model == 0:
+            return part.at[0, z_to // 2, 2 * (z_to % 2) + e]
+        return part.at[1, 2 * (z_to % 2) + e, z_to // 2]
+
+    ring_first = copies.take(28)
+    sent_ring = {}
+
+    def ring_step(model, k):
+        for e, step in ((0, 1), (1, -1)):
+            z_to = (z - step * (1 + k) + 2 * ZS) % ZS
+            if k == 0:
+                src = piece(model, z_to, e)
+            else:
+                sent_ring[model, e, k - 1].wait_recv()
+                src = ring.at[model, e, k - 1]
+                src[...] = (
+                    src[...].astype(jnp.float32) + piece(model, z_to, e)[...].astype(jnp.float32)
+                ).astype(src.dtype)
+            copy = start(
+                copies.remote(
+                    src,
+                    ring.at[model, e, k],
+                    ring_first + 14 * model + 7 * e + k,
+                    device(x, y, (z + step + ZS) % ZS, c),
+                )
+            )
+            sent_ring[model, e, k] = copy
+
+    def multiply(model, j):
+        total = None
+        for core in (0, 1):
+            tokens = nf[model, core].reshape(4 * rows, nf.shape[4])
+            term = jnp.dot(tokens, wf[model, j, core], preferred_element_type=jnp.float32)
+            total = term if total is None else total + term
+        part[model, :, j] = total.reshape(4, rows, total.shape[1]).astype(part.dtype)
+
+    fin_first = copies.take(8)
+    finals = []
+
+    def finish(model):
+        for e in (0, 1):
+            sent_ring[model, e, 6].wait_recv()
+            fin_src[model, e] = (
+                ring[model, e, 6].astype(jnp.float32)
+                + piece(model, z, e)[...].astype(jnp.float32)
+            ).astype(fin_src.dtype)
+            if model == 0:
+                target = device(x, 2 * (z % 2) + e, 2 * (z // 2) + y // 2, y % 2)
+                is_self = jnp.logical_and(
+                    jnp.logical_and(z % 2 == y // 2, c == y % 2), y % 2 == e
+                )
+            else:
+                target = device(z // 2, y, 2 * x + z % 2, e)
+                is_self = jnp.logical_and(z // 2 == x, c == e)
+            copy = pltpu.make_async_remote_copy(
+                src_ref=fin_src.at[model, e],
+                dst_ref=fin.at[model, c],
+                send_sem=send.at[fin_first + 4 * model + e],
+                recv_sem=recv.at[fin_first + 4 * model + c],
+                device_id=target,
+                device_id_type=MESH,
+            )
+            here = pltpu.make_async_copy(
+                fin_src.at[model, e], fin.at[model, c], local.at[5 + 2 * model + e]
+            )
+            pl.when(jnp.logical_not(is_self))(copy.start)
+            pl.when(is_self)(here.start)
+            finals.append((is_self, copy, here))
+
+    for model in (0, 1):
+        first, to_sibling = token_in[model]
+        to_sibling, forwards = token_forward[model]
+        token_own[model].wait()
+        to_sibling.wait_recv()
+        for copy in forwards:
+            copy.wait_recv()
+        for j in range(4):
+            multiply(model, j)
+            if model == 1 and j % 2 == 1:
+                ring_step(0, (j + 1) // 2)
+        ring_step(model, 0)
+
+    for k in range(3, 7):
+        ring_step(0, k)
+        ring_step(1, k - 2)
+    finish(0)
+    ring_step(1, 5)
+    ring_step(1, 6)
+
+    for i in range(16):
+        here = jnp.logical_and(seq == head, head == i)
+        arrived = pltpu.make_async_remote_copy(
+            src_ref=ss_ref,
+            dst_ref=sums.at[i],
+            send_sem=send.at[sums_first + i],
+            recv_sem=recv.at[sums_first + i],
+            device_id=sibling,
+            device_id_type=MESH,
+        )
+        pl.when(here)(sums_local.wait)
+        pl.when(jnp.logical_not(here))(arrived.wait_recv)
+    mean_square = jnp.sum(sums[...], axis=0) / 16384.0
+    scale = lax.rsqrt(mean_square + 1e-05)
+    columns = jnp.concatenate([scale] * 16, axis=0).T
+
+    finish(1)
+    for model in (0, 1):
+        for core in (0, 1):
+            if model == 0:
+                from_self = jnp.logical_and(
+                    jnp.logical_and(z % 2 == y // 2, c == y % 2), c == core
+                )
+                e = y % 2
+            else:
+                from_self = jnp.logical_and(z // 2 == x, c == core)
+                e = c
+            arrived = copies.remote(
+                fin_src.at[model, 0], fin.at[model, core], fin_first + 4 * model + core, sibling
+            )
+            pl.when(jnp.logical_not(from_self))(arrived.wait_recv)
+
+            @pl.when(from_self)
+            def _():
+                pltpu.make_async_copy(
+                    fin_src.at[model, 0], fin.at[model, core], local.at[5 + 2 * model + e]
+                ).wait()
+
+            out_ref[model, core * rows : (core + 1) * rows] = (
+                fin[model, core].astype(jnp.float32)
+                * columns[:, 2 * model + core : 2 * model + core + 1]
+            ).astype(out_ref.dtype)
+
+    for copy in started:
+        copy.wait_send()
+    for i, copy in enumerate(sums_sent):
+        if i == 0:
+            pl.when(head != seq)(copy.wait_send)
+        else:
+            copy.wait_send()
+    for is_self, copy, here in finals:
+        pl.when(jnp.logical_not(is_self))(copy.wait_send)
+
+
+def tail(normed, squares, w_out):
+    depth, width = w_out.shape[1], w_out.shape[2]
+    rows = normed.shape[1] // 2
+    packed = jnp.pad(squares.reshape(4, 128), ((0, 4), (0, 0)))
+    vmem = pl.BlockSpec(memory_space=pltpu.VMEM)
+    count = 120
+    return pl.pallas_call(
+        tail_kernel,
+        out_shape=jax.ShapeDtypeStruct((2, 2 * rows, width), jnp.bfloat16),
+        in_specs=[vmem, vmem, pl.BlockSpec(memory_space=pl.ANY)],
+        out_specs=vmem,
+        scratch_shapes=[
+            pltpu.VMEM((2, 4, 2, depth, width), jnp.bfloat16),
+            pltpu.VMEM((2, 2, 4, rows, depth), jnp.bfloat16),
+            pltpu.VMEM((2, 4, 4, rows, width), jnp.bfloat16),
+            pltpu.VMEM((2, 2, 7, rows, width), jnp.bfloat16),
+            pltpu.VMEM((2, 2, rows, width), jnp.bfloat16),
+            pltpu.VMEM((2, 2, rows, width), jnp.bfloat16),
+            pltpu.VMEM((16, 8, 128), jnp.float32),
+            pltpu.SemaphoreType.DMA((count,)),
+            pltpu.SemaphoreType.DMA((count,)),
+            pltpu.SemaphoreType.DMA((9,)),
+        ],
+        compiler_params=pltpu.CompilerParams(
+            has_side_effects=True, vmem_limit_bytes=60 * 1024 * 1024
+        ),
+    )(normed, packed, w_out)
 
 
 def local(
@@ -112,21 +497,9 @@
     gated = ssd_out.reshape(2, rows, local_heads * head_size) * jax.nn.silu(
         gate_z.astype(jnp.float32)
     )
-    square_sum = lax.psum(jnp.sum(gated * gated, axis=2), "head")
-    mean_square = square_sum / (HEADS * HEADDIM)
-    normed = (gated * lax.rsqrt(mean_square + 1e-05)[:, :, None] * norm_gain[:, None, :]).astype(
-        jnp.bfloat16
-    )
-    partial_terms = jnp.einsum(
-        "mtk,mkd->mtd",
-        lax.all_gather(normed, "seq", axis=1, tiled=True),
-        w_out,
-        preferred_element_type=jnp.float32,
-    )
-    summed = lax.psum_scatter(
-        partial_terms.astype(jnp.bfloat16), "head", scatter_dimension=1, tiled=True
-    )
-    return summed
+    squares = jnp.sum(gated * gated, axis=2)
+    raised = (gated * norm_gain[:, None, :]).astype(jnp.bfloat16)
+    return tail(raised, squares, w_out)
 
 
 def solution(mesh):

time: 310 us -> 216 us (0.70)
  waiting for transfers between devices: 200 us -> 8.67 us
  Pallas kernels: 0 us -> 156 us
  blocking collectives: 25.5 us -> 0 us
  matrix products: 28.5 us -> 10.2 us
  between operations: 13.6 us -> 0.27 us
    pallas_call x0 -> x1, Pallas kernels: none -> 156 us  [tail(): pl.pallas_call(tail_kernel, out_shape=jax.ShapeDtypeStruct((2, 2 * rows,...]
    all_gather x1 -> x0, waiting for transfers between devices: 125 us -> none  [local(): lax.all_gather(normed, 'seq', axis=1, tiled=True)]
    reduce_scatter x1 -> x0, waiting for transfers between devices: 66.5 us -> none  [local(): lax.psum_scatter(partial_terms.astype(jnp.bfloat16), 'head', scatter_dime...]
    psum x1 -> x0, blocking collectives: 25.5 us -> none  [local(): square_sum = lax.psum(jnp.sum(gated * gated, axis=2), 'head')]
    dot_general x1 -> x0, matrix products: 16.9 us -> none  [local(): jnp.einsum('mtk,mkd->mtd', lax.all_gather(normed, 'seq', axis=1, tiled=Tr...]
    convert_element_type x1 -> x0, other arithmetic: 3.3 us -> none  [local(): (gated * lax.rsqrt(mean_square + 1e-05)[:, :, None] * norm_gain[:, None,...]
  transfers between devices with their start and end apart: 8 -> 6, of which waited for: 5 -> 3; matrix products, arithmetic and copies ran while one was open for 4% -> 6% of each run, Pallas kernels for 0% -> 0%
where the time goes in v2:
time: 216 us; the launch traced here: 212 us
  Pallas kernels  156 us (72%)
  starting transfers between devices  19.7 us (9%)
  matrix products  10.2 us (5%)
  waiting for transfers between devices  8.67 us (4%)
  other arithmetic  8.53 us (4%)
  local copies, waits for them, and re-layouts  8.26 us (4%)
    pallas_call x1, Pallas kernels, tail(): pl.pallas_call(tail_kernel, out_shape=jax.ShapeDtypeStruct((2, 2 * rows,...  156 us
    ppermute x6, starting transfers between devices, passed_along(): return lax.ppermute(block, axis, route)  19.7 us
    ppermute x6, waiting for transfers between devices, passed_along(): return lax.ppermute(block, axis, route)  8.67 us
    dot_general x1, matrix products, span_output(): inside = jnp.einsum('mhij,mjhp->mihp', weights, x_block, precision=highest)  6.28 us
  transfers between devices with their start and end apart: 6, of which 3 were waited for; matrix products, arithmetic and copies ran while one was open for 6% of the time, Pallas kernels for 0%

profile of v2, /device:TPU:41, one launch (start us, length us, event | category | flops | bytes accessed | tf_op | source)
XLA Modules:
  0.0 212.1 jit_solution(18424199250253797345)
XLA Ops:
  0.0 1.3 slice.25
  1.3 3.2 %collective-permute-start = (s32[1]{0:T(128)}, s32[1]{0:T(128)}, u32[]{:S(2)}, u32[]{:S(2)}) collective-permute-start(s32[1]{0:T(128)} %slice.25), channel_id=1, source_target_pairs={{0,16},{16,32},{32,48},{48,64},{64,80},{80,96},{96,112},{112,128},... | collective-permute-start | bytes 20 | tf_op jit(solution)/shard_map/ppermute | solution.py:19
  4.5 0.7 neg.12
  5.2 0.8 copy_bitcast_fusion.1
  6.1 1.2 reduce-window.6
  7.7 1.5 copy.17
  9.5 1.3 compare_convert_fusion.1
  11.3 0.7 multiply_multiply_fusion.1
  12.1 1.2 fusion.39
  13.3 2.9 %collective-permute-start.1 = (bf16[2,16,64,128]{3,2,1,0:T(8,128)(2,1)S(1)}, bf16[2,16,64,128]{3,2,1,0:T(8,128)(2,1)S(1)}, u32[]{:S(2)}, u32[]{:S(2)}) collective-permute-start(bf16[2,16,64,128]{3,2,1,0:T(8,128)(2,1)S(1)} %get-tuple-element.38), channel_id=1, source_target_pairs={{0,16},{16,32},{32,48},{48,64},{64,80},{80,96},{96,112},{112,128},... | collective-permute-start | bytes 1572872 | tf_op jit(solution)/shard_map/ppermute | solution.py:19
  16.4 1.0 fusion.28
  17.5 3.8 %collective-permute-start.4 = (f32[2,16]{1,0:T(2,128)S(1)}, f32[2,16]{1,0:T(2,128)S(1)}, u32[]{:S(2)}, u32[]{:S(2)}) collective-permute-start(f32[2,16]{1,0:T(2,128)S(1)} %slice_reduce_fusion.1), channel_id=1, source_target_pairs={{0,32},{16,48},{32,64},{48,80},{64,96},{80,112},{96,128},{112,144}... | collective-permute-start | bytes 392 | tf_op jit(solution)/shard_map/ppermute | solution.py:19
  21.3 2.6 %collective-permute-start.3 = (f32[2,16]{1,0:T(2,128)S(1)}, f32[2,16]{1,0:T(2,128)S(1)}, u32[]{:S(2)}, u32[]{:S(2)}) collective-permute-start(f32[2,16]{1,0:T(2,128)S(1)} %slice_reduce_fusion.1), channel_id=1, source_target_pairs={{0,16},{16,32},{32,48},{48,64},{64,80},{80,96},{96,112},{112,128},... | collective-permute-start | bytes 392 | tf_op jit(solution)/shard_map/ppermute | solution.py:19
  23.9 3.9 %collective-permute-done.1 = bf16[2,16,64,128]{3,2,1,0:T(8,128)(2,1)S(1)} collective-permute-done((bf16[2,16,64,128]{3,2,1,0:T(8,128)(2,1)S(1)}, bf16[2,16,64,128]{3,2,1,0:T(8,128)(2,1)S(1)}, u32[]{:S(2)}, u32[]{:S(2)}) %collective-permute-start.1) | collective-permute-done | bytes 524320 | tf_op jit(solution)/shard_map/ppermute | solution.py:19
  28.0 5.1 %collective-permute-start.5 = (bf16[2,16,64,128]{3,2,1,0:T(8,128)(2,1)S(1)}, bf16[2,16,64,128]{3,2,1,0:T(8,128)(2,1)S(1)}, u32[]{:S(2)}, u32[]{:S(2)}) collective-permute-start(bf16[2,16,64,128]{3,2,1,0:T(8,128)(2,1)S(1)} %add_convert_fusion), channel_id=1, source_target_pairs={{0,48},{16,64},{32,80},{48,96},{64,112},{80,128},{96,144},{112,160... | collective-permute-start | bytes 1572872 | tf_op jit(solution)/shard_map/ppermute | solution.py:19
  33.1 2.1 collective-permute-start.2
  35.2 6.3 %fusion = f32[2,16,256,64]{2,3,1,0:T(8,128)S(1)} fusion(bf16[2,256,16,64]{1,3,2,0:T(8,128)(2,1)S(1)} %bitcast.61, f32[2,16,256]{2,1,0:T(8,128)S(1)} %get-tuple-element.32, f32[2,256,256]{2,1,0:T(8,128)S(1)} %fusion.40, f32[256,256]{1,0:T(8,128)S(1)} %fusion.31, f32[2,16,256]{2,1,0:T(8,128)S(1)} %get-tuple-element.35), kind=kOutput, calls=%fused_computation | convolution fusion | flops 1621098496 | bytes 3997696 | tf_op jit(solution)/shard_map/while/body/eval_jaxpr/mhij,mjhp->mihp/dot_general | solution.py:62
  41.6 0.9 collective-permute-done.5
  42.5 3.9 %collective-permute-done.2 = bf16[2,16,64,128]{3,2,1,0:T(8,128)(2,1)S(1)} collective-permute-done((bf16[2,16,64,128]{3,2,1,0:T(8,128)(2,1)S(1)}, bf16[2,16,64,128]{3,2,1,0:T(8,128)(2,1)S(1)}, u32[]{:S(2)}, u32[]{:S(2)}) %collective-permute-start.2) | collective-permute-done | bytes 524320 | tf_op jit(solution)/shard_map/ppermute | solution.py:19
  46.4 1.5 fusion.14
  47.9 1.9 copy.18
  49.8 3.4 %multiply_reduce_fusion = (f32[2,256]{1,0:T(2,128)S(1)}, bf16[2,256,1024]{2,1,0:T(8,128)(2,1)}) fusion(f32[2,256,1024]{2,1,0:T(8,128)} %copy.18, bf16[2,256,1024]{2,1,0:T(8,128)(2,1)S(1)} %copy-done.1, f32[2,1024]{1,0:T(2,128)S(1)} %copy-done.5), kind=kLoop, calls=%fused_computation.27 | loop fusion | flops 5242368 | bytes 4204544 | tf_op jit(solution)/shard_map/reduce_sum | solution.py:500
  53.8 156.4 %shard_map.109 = bf16[2,256,512]{2,1,0:T(8,128)(2,1)} custom-call(bf16[2,256,1024]{2,1,0:T(8,128)(2,1)} %get-tuple-element.30.n_ref, f32[8,128]{1,0:T(8,128)} %pad.4.ss_ref, bf16[2,1024,512]{2,1,0:T(8,128)(2,1)} %w_ref.1), custom_call_target="tpu_custom_call" | custom-call | tf_op jit(solution)/shard_map/pallas_call | solution.py:427
  210.2 1.9 copy.32
  (33 shorter events, 2.5 us)
Async XLA Ops:
  0.0 9.2 %copy-start = (bf16[2,256,128]{2,1,0:T(8,128)(2,1)S(1)}, bf16[2,256,128]{2,1,0:T(8,128)(2,1)}, u32[]{:S(2)}) copy-start(bf16[2,256,128]{2,1,0:T(8,128)(2,1)} %param.14) | copy-start | bytes 393220
  0.0 9.5 %copy-start.4 = (s32[256]{0:T(256)S(1)}, s32[256]{0:T(256)}, u32[]{:S(2)}) copy-start(s32[256]{0:T(256)} %param.21) | copy-start | bytes 3076
  0.0 12.0 %copy-start.6 = (f32[2,16]{1,0:T(2,128)S(1)}, f32[2,16]{1,0:T(2,128)}, u32[]{:S(2)}) copy-start(f32[2,16]{1,0:T(2,128)} %param.16) | copy-start | bytes 388
  0.0 12.0 %copy-start.3 = (f32[2,256,16]{1,2,0:T(8,128)S(1)}, f32[2,256,16]{1,2,0:T(8,128)}, u32[]{:S(2)}) copy-start(f32[2,256,16]{1,2,0:T(8,128)} %param.15) | copy-start | bytes 98308
  0.0 9.2 %copy-start.2 = (bf16[2,256,128]{2,1,0:T(8,128)(2,1)S(1)}, bf16[2,256,128]{2,1,0:T(8,128)(2,1)}, u32[]{:S(2)}) copy-start(bf16[2,256,128]{2,1,0:T(8,128)(2,1)} %param.13) | copy-start | bytes 393220
  1.3 8.1 %collective-permute-start = (s32[1]{0:T(128)}, s32[1]{0:T(128)}, u32[]{:S(2)}, u32[]{:S(2)}) collective-permute-start(s32[1]{0:T(128)} %slice.25), channel_id=1, source_target_pairs={{0,16},{16,32},{32,48},{48,64},{64,80},{80,96},{96,112},{112,128},... | collective-permute-start | bytes 20 | tf_op jit(solution)/shard_map/ppermute | solution.py:19
  13.3 14.4 %collective-permute-start.1 = (bf16[2,16,64,128]{3,2,1,0:T(8,128)(2,1)S(1)}, bf16[2,16,64,128]{3,2,1,0:T(8,128)(2,1)S(1)}, u32[]{:S(2)}, u32[]{:S(2)}) collective-permute-start(bf16[2,16,64,128]{3,2,1,0:T(8,128)(2,1)S(1)} %get-tuple-element.38), channel_id=1, source_target_pairs={{0,16},{16,32},{32,48},{48,64},{64,80},{80,96},{96,112},{112,128},... | collective-permute-start | bytes 1572872 | tf_op jit(solution)/shard_map/ppermute | solution.py:19
  17.5 24.0 %collective-permute-start.4 = (f32[2,16]{1,0:T(2,128)S(1)}, f32[2,16]{1,0:T(2,128)S(1)}, u32[]{:S(2)}, u32[]{:S(2)}) collective-permute-start(f32[2,16]{1,0:T(2,128)S(1)} %slice_reduce_fusion.1), channel_id=1, source_target_pairs={{0,32},{16,48},{32,64},{48,80},{64,96},{80,112},{96,128},{112,144}... | collective-permute-start | bytes 392 | tf_op jit(solution)/shard_map/ppermute | solution.py:19
  21.3 20.2 %collective-permute-start.3 = (f32[2,16]{1,0:T(2,128)S(1)}, f32[2,16]{1,0:T(2,128)S(1)}, u32[]{:S(2)}, u32[]{:S(2)}) collective-permute-start(f32[2,16]{1,0:T(2,128)S(1)} %slice_reduce_fusion.1), channel_id=1, source_target_pairs={{0,16},{16,32},{32,48},{48,64},{64,80},{80,96},{96,112},{112,128},... | collective-permute-start | bytes 392 | tf_op jit(solution)/shard_map/ppermute | solution.py:19
  28.0 14.5 %collective-permute-start.5 = (bf16[2,16,64,128]{3,2,1,0:T(8,128)(2,1)S(1)}, bf16[2,16,64,128]{3,2,1,0:T(8,128)(2,1)S(1)}, u32[]{:S(2)}, u32[]{:S(2)}) collective-permute-start(bf16[2,16,64,128]{3,2,1,0:T(8,128)(2,1)S(1)} %add_convert_fusion), channel_id=1, source_target_pairs={{0,48},{16,64},{32,80},{48,96},{64,112},{80,128},{96,144},{112,160... | collective-permute-start | bytes 1572872 | tf_op jit(solution)/shard_map/ppermute | solution.py:19
  33.1 13.2 %collective-permute-start.2 = (bf16[2,16,64,128]{3,2,1,0:T(8,128)(2,1)S(1)}, bf16[2,16,64,128]{3,2,1,0:T(8,128)(2,1)S(1)}, u32[]{:S(2)}, u32[]{:S(2)}) collective-permute-start(bf16[2,16,64,128]{3,2,1,0:T(8,128)(2,1)S(1)} %add_convert_fusion), channel_id=1, source_target_pairs={{0,16},{16,32},{32,48},{48,64},{64,80},{80,96},{96,112},{112,128},... | collective-permute-start | bytes 1572872 | tf_op jit(solution)/shard_map/ppermute | solution.py:19
  35.2 11.1 %copy-start.7 = (f32[2,16]{1,0:T(2,128)S(1)}, f32[2,16]{1,0:T(2,128)}, u32[]{:S(2)}) copy-start(f32[2,16]{1,0:T(2,128)} %param.18) | copy-start | bytes 388
  47.9 1.9 copy-start.1
  47.9 1.9 copy-start.5

commit v3 on v2

v3 whole, which is shorter than its diff:
```python
import jax
import jax.numpy as jnp
from jax import lax
from jax.experimental import pallas as pl
from jax.experimental.pallas import tpu as pltpu
from jax.sharding import PartitionSpec as P

highest = lax.Precision.HIGHEST
FAR = -1e30

MESH = pl.DeviceIdType.MESH
XS, YS, ZS = 4, 4, 8


class Copies:
    def __init__(self, send, recv):
        self.send, self.recv, self.used = send, recv, 0

    def take(self, count=1):
        first = self.used
        self.used += count
        return first

    def remote(self, src, dst, slot, device):
        return pltpu.make_async_remote_copy(
            src_ref=src,
            dst_ref=dst,
            send_sem=self.send.at[slot],
            recv_sem=self.recv.at[slot],
            device_id=device,
            device_id_type=MESH,
        )


def layer_kernel(
    x_hbm, g_hbm, b_ref, c_ref, dt_ref, bias_ref, rate_ref, skip_ref, gain_ref, seg_ref, w_ref,
    out_ref,
    xv, gv, n_ref, ss_ref, inner, mask, products, spread, seg_own, seg_before,
    local_state, state_out, state_in, pair_out, pair_in, decay_out, decay_in,
    wf, nf, part, ring, fin_src, fin, sums, send, recv, local,
):
    seq, head = lax.axis_index("seq"), lax.axis_index("head")
    x, y = seq // YS, seq % YS
    z, c = head // 2, head % 2
    other = 1 - c

    def device(x_at, y_at, z_at, c_at):
        return {"seq": x_at * YS + y_at, "head": z_at * 2 + c_at}

    copies = Copies(send, recv)
    started = []

    def start(copy):
        copy.start()
        started.append(copy)
        return copy

    sibling = device(x, y, z, other)

    def weight_at(model):
        return y if model == 0 else x

    def weight_peer(model, step):
        if model == 0:
            return device(x, (y + step) % YS, z, c)
        return device((x + step) % XS, y, z, c)

    def token_at(model):
        return x if model == 0 else y

    def token_peer(model, step, core):
        if model == 0:
            return device((x + step) % XS, y, z, core)
        return device(x, (y + step) % YS, z, core)

    half = wf.shape[3] // 2
    rows = nf.shape[3]
    tokens, lanes = xv.shape[1], xv.shape[2]
    heads = dt_ref.shape[2]
    upper, lower = pl.ds(0, half), pl.ds(half, half)

    x_copy = pltpu.make_async_copy(x_hbm, xv, local.at[9])
    g_copy = pltpu.make_async_copy(g_hbm, gv, local.at[10])
    x_copy.start()

    def follower(distance):
        return {"seq": (seq + distance) % 16, "head": head}

    seg_row = seg_ref[...].astype(jnp.float32)
    seg_own[...] = jnp.broadcast_to(seg_row, seg_own.shape)
    seg_copy = start(copies.remote(seg_own, seg_before, copies.take(), follower(1)))

    weights_in = []
    own_local = []
    weight_slot = [copies.take(5) for model in (0, 1)]
    order = ((1, upper, 0), (-1, lower, 1), (1, lower, 2), (-1, upper, 3))

    def send_weights(model, which):
        at = weight_at(model)
        for step, part_rows, n in order:
            if n in which:
                copy = start(
                    copies.remote(
                        w_ref.at[model, part_rows],
                        wf.at[model, at, c, part_rows],
                        weight_slot[model] + n,
                        weight_peer(model, step),
                    )
                )
                weights_in.append((model, step, part_rows, n, copy))

    send_weights(1, (0, 1))
    send_weights(0, (1,))
    send_weights(1, (2, 3))
    send_weights(0, (3,))
    g_copy.start()
    forward_later = []
    for model in (0, 1):
        at = weight_at(model)
        own = pltpu.make_async_copy(w_ref.at[model], wf.at[model, at, c], local.at[model])
        own.start()
        own_local.append(own)
        forward_later.append(
            start(
                copies.remote(
                    w_ref.at[model], wf.at[model, at, c], weight_slot[model] + 4, sibling
                )
            )
        )

    row_at = lax.broadcasted_iota(jnp.int32, (tokens, tokens), 0)
    col_at = lax.broadcasted_iota(jnp.int32, (tokens, tokens), 1)
    eye = (row_at == col_at).astype(jnp.float32)
    lower_ones = (row_at >= col_at).astype(jnp.float32)
    seg_col = lax.dot_general(
        eye, seg_own[...], (((1,), (1,)), ((), ())), precision=highest
    )[:, 0:1]
    mask[...] = jnp.where(
        jnp.logical_and(row_at >= col_at, jnp.abs(seg_col - seg_row) < 0.5), 0.0, FAR
    )
    spread[...] = (
        lax.broadcasted_iota(jnp.int32, spread.shape, 0)
        == lax.broadcasted_iota(jnp.int32, spread.shape, 1) // (lanes // heads)
    ).astype(spread.dtype)
    same_last = (jnp.abs(seg_col - seg_row[:, tokens - 1 : tokens]) < 0.5).astype(jnp.float32)

    def widen(values, columns):
        coarse = values.astype(jnp.bfloat16)
        fine = (values - coarse.astype(jnp.float32)).astype(jnp.bfloat16)
        table = spread[:, columns]
        return jnp.dot(coarse, table, preferred_element_type=jnp.float32) + jnp.dot(
            fine, table, preferred_element_type=jnp.float32
        )

    blocks = [pl.ds(start_at, 256) for start_at in range(0, lanes, 256)]
    state_first = copies.take(2)
    state_copies, running, shifted, totals = [], [], [], []
    x_copy.wait()
    for model in (0, 1):
        raw = dt_ref[model] + bias_ref[model : model + 1, :]
        step_size = jnp.maximum(raw, 0.0) + jnp.log1p(jnp.exp(-jnp.abs(raw)))
        log_decay = -(rate_ref[model : model + 1, :] * step_size)
        run = jnp.dot(lower_ones, log_decay, precision=highest)
        total = run[tokens - 1 : tokens, :]
        tail_w = jnp.exp(total - run) * same_last * step_size
        for block in blocks:
            weighted = (xv[model, :, block].astype(jnp.float32) * widen(tail_w, block)).astype(
                jnp.bfloat16
            )
            fresh = lax.dot_general(
                b_ref[model],
                weighted,
                (((0,), (0,)), ((), ())),
                preferred_element_type=jnp.float32,
            )
            local_state[model, :, block] = fresh
            state_out[model, :, block] = fresh.astype(jnp.bfloat16)
        state_copies.append(
            start(
                copies.remote(
                    state_out.at[model], state_in.at[model], state_first + model, follower(1)
                )
            )
        )
        running.append(run)
        totals.append(total)
        shifted.append(run - jnp.log(step_size))
    send_weights(0, (0,))

    seg_copy.wait_recv()
    anchor = seg_before[0:1, tokens - 1 : tokens]
    has_before = jnp.where(seq > 0, 1.0, 0.0)
    entered = (jnp.abs(seg_col - anchor) < 0.5).astype(jnp.float32) * has_before
    for model in (0, 1):
        kept = jnp.exp(totals[model]) * entered[tokens - 1 : tokens, :]
        kept = jnp.broadcast_to(kept, (8, heads))
        for block in blocks:
            decay_out[model, :, block] = widen(kept, block)
    decay_first = copies.take(2)
    decay_copies = [
        start(copies.remote(decay_out, decay_in.at[i], decay_first + i, follower(i + 1)))
        for i in (0, 1)
    ]

    def inside(model):
        run = running[model]
        shifted_t = lax.dot_general(
            shifted[model], eye, (((0,), (0,)), ((), ())), precision=highest
        )
        products[...] = lax.dot_general(
            c_ref[model],
            b_ref[model],
            (((1,), (1,)), ((), ())),
            preferred_element_type=jnp.float32,
        )
        lane = lax.broadcasted_iota(jnp.int32, (1, 128), 1)
        skip = jnp.broadcast_to(skip_ref[model : model + 1, :], (8, heads))
        mid = tokens // 2
        for pair in range(heads // 2):
            columns = pl.ds(128 * pair, 128)
            x_pair = xv[model, :, columns]
            early = late = None
            for q in (0, 1):
                h = 2 * pair + q
                x_one = x_pair * (lane // 64 == q).astype(jnp.bfloat16)
                gap = run[:mid, h : h + 1] - shifted_t[h : h + 1, :mid] + mask[:mid, :mid]
                weights = (jnp.exp(gap) * products[:mid, :mid]).astype(jnp.bfloat16)
                term = jnp.dot(weights, x_one[:mid], preferred_element_type=jnp.float32)
                early = term if early is None else early + term
                gap = run[mid:, h : h + 1] - shifted_t[h : h + 1, :] + mask[mid:, :]
                weights = (jnp.exp(gap) * products[mid:, :]).astype(jnp.bfloat16)
                term = jnp.dot(weights, x_one, preferred_element_type=jnp.float32)
                late = term if late is None else late + term
            passed = x_pair.astype(jnp.float32) * widen(skip, columns)[0:1, :]
            inner[model, :mid, columns] = early + passed[:mid]
            inner[model, mid:, columns] = late + passed[mid:]

    pair_first = copies.take(4)
    pair_copies = []

    def join_pair(model):
        state_copies[model].wait_recv()
        for block in blocks:
            pair_out[model, :, block] = (
                local_state[model, :, block]
                + decay_out[model, 0:1, block] * state_in[model, :, block].astype(jnp.float32)
            ).astype(jnp.bfloat16)
        pair_copies.append(
            [
                start(
                    copies.remote(
                        pair_out.at[model],
                        pair_in.at[model, i],
                        pair_first + 2 * model + i,
                        follower(1 + 2 * i),
                    )
                )
                for i in (0, 1)
            ]
        )

    def gate(model):
        entry_w = jnp.exp(running[model]) * entered
        squares = jnp.zeros((tokens, 128), jnp.float32)
        for copy in pair_copies[model]:
            copy.wait_recv()
        for block in blocks:
            earlier = pair_in[model, 0, :, block].astype(jnp.float32) + (
                decay_in[0, model, 0:1, block] * decay_in[1, model, 0:1, block]
            ) * pair_in[model, 1, :, block].astype(jnp.float32)
            entering = jnp.dot(
                c_ref[model], earlier.astype(jnp.bfloat16), preferred_element_type=jnp.float32
            )
            ssd_out = inner[model, :, block] + widen(entry_w, block) * entering
            opened = gv[model, :, block].astype(jnp.float32)
            gated = ssd_out * (opened / (1.0 + jnp.exp(-opened)))
            squares = squares + (
                gated[:, :128] * gated[:, :128] + gated[:, 128:] * gated[:, 128:]
            )
            n_ref[model, :, block] = (gated * gain_ref[model : model + 1, block]).astype(
                jnp.bfloat16
            )
        sums_row = lax.dot_general(
            jnp.ones((8, 128), jnp.float32),
            squares,
            (((1,), (1,)), ((), ())),
            precision=highest,
        )
        ss_ref[2 * model : 2 * model + 1, :] = sums_row[0:1, :128]
        ss_ref[2 * model + 1 : 2 * model + 2, :] = sums_row[0:1, 128:]

    inside(0)
    join_pair(0)
    inside(1)
    join_pair(1)
    send_weights(0, (2,))
    g_copy.wait()
    for copy in decay_copies:
        copy.wait_recv()
    ss_ref[...] = jnp.zeros_like(ss_ref)

    token_in = {}
    token_own = []
    size = YS

    def send_tokens(model):
        at = token_at(model)
        mine = pl.ds(pl.multiple_of(c * rows, rows), rows)
        theirs = pl.ds(pl.multiple_of(other * rows, rows), rows)
        own = pltpu.make_async_copy(n_ref.at[model, mine], nf.at[model, c, at], local.at[3 + model])
        own.start()
        token_own.append(own)
        first = copies.take(8)
        to_sibling = start(
            copies.remote(n_ref.at[model, theirs], nf.at[model, c, at], first + 4, sibling)
        )
        sends = []
        for core in (0, 1):
            for n, step in ((0, 1), (1, -1)):
                piece = n_ref.at[model, pl.ds(core * rows, rows)]
                copy = pltpu.make_async_remote_copy(
                    src_ref=piece,
                    dst_ref=nf.at[model, c, at],
                    send_sem=send.at[first + 2 * core + n],
                    recv_sem=recv.at[first + 2 * c + n],
                    device_id=token_peer(model, step, core),
                    device_id_type=MESH,
                )
                sends.append(start(copy))
        token_in[model] = (first, to_sibling)

    def arrival(dst, slot):
        return copies.remote(dst, dst, slot, sibling)

    sibling_waits = []
    opposite = []

    def forward_weights(model, which):
        at = weight_at(model)
        for step, part_rows, n, copy in [w[1:] for w in weights_in if w[0] == model]:
            if n not in which:
                continue
            source = (at - step + size) % size
            copy.wait_recv()
            held = wf.at[model, source, c, part_rows]
            if n < 2:
                onward = start(
                    copies.remote(held, held, copies.take(), weight_peer(model, step))
                )
                opposite.append((model, step, part_rows, onward))
            sibling_waits.append(start(copies.remote(held, held, copies.take(), sibling)))

    def forward_opposite():
        for model, step, part_rows, onward in opposite:
            at = weight_at(model)
            source = (at - 2 * step + 2 * size) % size
            onward.wait_recv()
            held = wf.at[model, source, c, part_rows]
            sibling_waits.append(start(copies.remote(held, held, copies.take(), sibling)))

    token_forward = {}

    def forward_tokens(model):
        at = token_at(model)
        first, to_sibling = token_in[model]
        forwards = []
        for core, n, step in ((0, 0, 1), (1, 1, -1), (1, 0, 1), (0, 1, -1)):
            source = (at - step + size) % size
            arrival(nf.at[model, core, source], first + 2 * core + n).wait_recv()
            if core == n:
                forwards.append(
                    start(
                        copies.remote(
                            nf.at[model, core, source],
                            nf.at[model, core, source],
                            first + 5 + n,
                            token_peer(model, step, c),
                        )
                    )
                )
        token_forward[model] = (to_sibling, forwards)

    forward_weights(1, (0, 1))
    forward_weights(0, (1,))
    forward_weights(1, (2, 3))
    forward_weights(0, (3,))
    gate(0)
    send_tokens(0)
    gate(1)
    send_tokens(1)
    sums_first = copies.take(16)
    sums_local = pltpu.make_async_copy(ss_ref, sums.at[head], local.at[2])
    sums_sent = []
    for i in range(16):
        copy = pltpu.make_async_remote_copy(
            src_ref=ss_ref,
            dst_ref=sums.at[head],
            send_sem=send.at[sums_first + i],
            recv_sem=recv.at[sums_first + head],
            device_id={"seq": (seq + i) % 16, "head": seq},
            device_id_type=MESH,
        )
        sums_sent.append(copy)
        if i == 0:
            pl.when(head != seq)(copy.start)
            pl.when(head == seq)(sums_local.start)
        else:
            copy.start()

    forward_weights(0, (0,))
    forward_tokens(0)
    forward_weights(0, (2,))
    forward_tokens(1)
    forward_opposite()
    for own in own_local:
        own.wait()
    for copy in forward_later + sibling_waits:
        copy.wait_recv()

    def piece(model, z_to, e):
        if model == 0:
            return part.at[0, z_to // 2, 2 * (z_to % 2) + e]
        return part.at[1, 2 * (z_to % 2) + e, z_to // 2]

    ring_first = copies.take(28)
    sent_ring = {}

    def ring_step(model, k):
        for e, step in ((0, 1), (1, -1)):
            z_to = (z - step * (1 + k) + 2 * ZS) % ZS
            if k == 0:
                src = piece(model, z_to, e)
            else:
                sent_ring[model, e, k - 1].wait_recv()
                src = ring.at[model, e, k - 1]
                src[...] = (
                    src[...].astype(jnp.float32) + piece(model, z_to, e)[...].astype(jnp.float32)
                ).astype(src.dtype)
            copy = start(
                copies.remote(
                    src,
                    ring.at[model, e, k],
                    ring_first + 14 * model + 7 * e + k,
                    device(x, y, (z + step + ZS) % ZS, c),
                )
            )
            sent_ring[model, e, k] = copy

    def multiply(model, j):
        total = None
        for core in (0, 1):
            tokens = nf[model, core].reshape(4 * rows, nf.shape[4])
            term = jnp.dot(tokens, wf[model, j, core], preferred_element_type=jnp.float32)
            total = term if total is None else total + term
        part[model, :, j] = total.reshape(4, rows, total.shape[1]).astype(part.dtype)

    fin_first = copies.take(8)
    finals = []

    def finish(model):
        for e in (0, 1):
            sent_ring[model, e, 6].wait_recv()
            fin_src[model, e] = (
                ring[model, e, 6].astype(jnp.float32)
                + piece(model, z, e)[...].astype(jnp.float32)
            ).astype(fin_src.dtype)
            if model == 0:
                target = device(x, 2 * (z % 2) + e, 2 * (z // 2) + y // 2, y % 2)
                is_self = jnp.logical_and(
                    jnp.logical_and(z % 2 == y // 2, c == y % 2), y % 2 == e
                )
            else:
                target = device(z // 2, y, 2 * x + z % 2, e)
                is_self = jnp.logical_and(z // 2 == x, c == e)
            copy = pltpu.make_async_remote_copy(
                src_ref=fin_src.at[model, e],
                dst_ref=fin.at[model, c],
                send_sem=send.at[fin_first + 4 * model + e],
                recv_sem=recv.at[fin_first + 4 * model + c],
                device_id=target,
                device_id_type=MESH,
            )
            here = pltpu.make_async_copy(
                fin_src.at[model, e], fin.at[model, c], local.at[5 + 2 * model + e]
            )
            pl.when(jnp.logical_not(is_self))(copy.start)
            pl.when(is_self)(here.start)
            finals.append((is_self, copy, here))

    for model in (0, 1):
        first, to_sibling = token_in[model]
        to_sibling, forwards = token_forward[model]
        token_own[model].wait()
        to_sibling.wait_recv()
        for copy in forwards:
            copy.wait_recv()
        for j in range(4):
            multiply(model, j)
            if model == 1 and j % 2 == 1:
                ring_step(0, (j + 1) // 2)
        ring_step(model, 0)

    for k in range(3, 7):
        ring_step(0, k)
        ring_step(1, k - 2)
    finish(0)
    ring_step(1, 5)
    ring_step(1, 6)

    for i in range(16):
        here = jnp.logical_and(seq == head, head == i)
        arrived = pltpu.make_async_remote_copy(
            src_ref=ss_ref,
            dst_ref=sums.at[i],
            send_sem=send.at[sums_first + i],
            recv_sem=recv.at[sums_first + i],
            device_id=sibling,
            device_id_type=MESH,
        )
        pl.when(here)(sums_local.wait)
        pl.when(jnp.logical_not(here))(arrived.wait_recv)
    mean_square = jnp.sum(sums[...], axis=0) / 16384.0
    scale = lax.rsqrt(mean_square + 1e-05)
    columns = jnp.concatenate([scale] * 16, axis=0).T

    finish(1)
    for model in (0, 1):
        for core in (0, 1):
            if model == 0:
                from_self = jnp.logical_and(
                    jnp.logical_and(z % 2 == y // 2, c == y % 2), c == core
                )
                e = y % 2
            else:
                from_self = jnp.logical_and(z // 2 == x, c == core)
                e = c
            arrived = copies.remote(
                fin_src.at[model, 0], fin.at[model, core], fin_first + 4 * model + core, sibling
            )
            pl.when(jnp.logical_not(from_self))(arrived.wait_recv)

            @pl.when(from_self)
            def _():
                pltpu.make_async_copy(
                    fin_src.at[model, 0], fin.at[model, core], local.at[5 + 2 * model + e]
                ).wait()

            out_ref[model, core * rows : (core + 1) * rows] = (
                fin[model, core].astype(jnp.float32)
                * columns[:, 2 * model + core : 2 * model + core + 1]
            ).astype(out_ref.dtype)

    for copy in started:
        copy.wait_send()
    for i, copy in enumerate(sums_sent):
        if i == 0:
            pl.when(head != seq)(copy.wait_send)
        else:
            copy.wait_send()
    for is_self, copy, here in finals:
        pl.when(jnp.logical_not(is_self))(copy.wait_send)


def local(
    x_heads, gate_z, b_proj, c_proj, dt_raw, dt_bias, decay_rate, skip_d, norm_gain, w_out, seg_ids
):
    tokens, lanes = x_heads.shape[1], x_heads.shape[2]
    depth, width = w_out.shape[1], w_out.shape[2]
    state, rows = b_proj.shape[2], tokens // 2
    bf16, f32 = jnp.bfloat16, jnp.float32
    vmem = pl.BlockSpec(memory_space=pltpu.VMEM)
    hbm = pl.BlockSpec(memory_space=pl.ANY)
    count = 128
    return pl.pallas_call(
        layer_kernel,
        out_shape=jax.ShapeDtypeStruct((2, tokens, width), bf16),
        in_specs=[hbm, hbm] + [vmem] * 8 + [hbm],
        out_specs=vmem,
        scratch_shapes=[
            pltpu.VMEM((2, tokens, lanes), bf16),
            pltpu.VMEM((2, tokens, lanes), bf16),
            pltpu.VMEM((2, tokens, lanes), bf16),
            pltpu.VMEM((8, 128), f32),
            pltpu.VMEM((2, tokens, lanes), f32),
            pltpu.VMEM((tokens, tokens), f32),
            pltpu.VMEM((tokens, tokens), f32),
            pltpu.VMEM((dt_raw.shape[2], lanes), bf16),
            pltpu.VMEM((8, tokens), f32),
            pltpu.VMEM((8, tokens), f32),
            pltpu.VMEM((2, state, lanes), f32),
            pltpu.VMEM((2, state, lanes), bf16),
            pltpu.VMEM((2, state, lanes), bf16),
            pltpu.VMEM((2, state, lanes), bf16),
            pltpu.VMEM((2, 2, state, lanes), bf16),
            pltpu.VMEM((2, 8, lanes), f32),
            pltpu.VMEM((2, 2, 8, lanes), f32),
            pltpu.VMEM((2, 4, 2, depth, width), bf16),
            pltpu.VMEM((2, 2, 4, rows, depth), bf16),
            pltpu.VMEM((2, 4, 4, rows, width), bf16),
            pltpu.VMEM((2, 2, 7, rows, width), bf16),
            pltpu.VMEM((2, 2, rows, width), bf16),
            pltpu.VMEM((2, 2, rows, width), bf16),
            pltpu.VMEM((16, 8, 128), f32),
            pltpu.SemaphoreType.DMA((count,)),
            pltpu.SemaphoreType.DMA((count,)),
            pltpu.SemaphoreType.DMA((11,)),
        ],
        compiler_params=pltpu.CompilerParams(
            has_side_effects=True, vmem_limit_bytes=62 * 1024 * 1024
        ),
    )(
        x_heads,
        gate_z,
        b_proj,
        c_proj,
        dt_raw,
        dt_bias,
        decay_rate,
        skip_d,
        norm_gain,
        seg_ids.reshape(1, tokens),
        w_out,
    )


def solution(mesh):
    placed = (
        P(None, "seq", "head"),
        P(None, "seq", "head"),
        P(None, "seq", None),
        P(None, "seq", None),
        P(None, "seq", "head"),
        P(None, "head"),
        P(None, "head"),
        P(None, "head"),
        P(None, "head"),
        P(None, "head", "seq"),
        P("seq"),
    )
    return jax.shard_map(
        local, mesh=mesh, in_specs=placed, out_specs=P(None, "head", "seq"), check_vma=False
    )
```

time: 216 us -> 192 us (0.89)
  the two profiles are of different devices: /device:TPU:41 before, /device:TPU:27 now
where the time goes in v3:
time: 192 us
  Pallas kernels  188 us (98%)
  local copies, waits for them, and re-layouts  3.46 us (2%)
    pallas_call x1, Pallas kernels, local(): pl.pallas_call(layer_kernel, out_shape=jax.ShapeDtypeStruct((2, tokens, w...  188 us

profile of v3, /device:TPU:27, one launch (start us, length us, event | category | flops | bytes accessed | tf_op | source)
XLA Modules:
  0.0 191.5 jit_solution(11193490868761076418)
XLA Ops:
  0.0 1.6 copy.12.dt_ref
  1.6 188.0 %shard_map.109 = bf16[2,256,512]{2,1,0:T(8,128)(2,1)} custom-call(bf16[2,256,1024]{2,1,0:T(8,128)(2,1)} %x_hbm.1, bf16[2,256,1024]{2,1,0:T(8,128)(2,1)} %g_hbm.1, bf16[2,256,128]{2,1,0:T(8,128)(2,1)} %b_ref.1, bf16[2,256,128]{2,1,0:T(8,128)(2,1)} %c_ref.1, f32[2,256,16]{2,1,0:T(8,128)} %copy.12.dt_ref, f32[2,16]{1,0:T(2,128)} %bias_ref.1, f32[2,16]{1,0:T(2,128)} %rate_ref.1, ...), custom_call_target="tpu_custom_call" | custom-call | tf_op jit(solution)/shard_map/pallas_call | solution.py:574
  189.6 1.9 copy.14

commit v4 on v3

v4 whole, which is shorter than its diff:
```python
import functools

import jax
import jax.numpy as jnp
from jax import lax
from jax.experimental import pallas as pl
from jax.experimental.pallas import tpu as pltpu
from jax.sharding import PartitionSpec as P

highest = lax.Precision.HIGHEST
FAR = -1e30

MESH = pl.DeviceIdType.MESH
XS, YS, ZS = 4, 4, 8


class Copies:
    def __init__(self, send, recv):
        self.send, self.recv, self.used = send, recv, 0

    def take(self, count=1):
        first = self.used
        self.used += count
        return first

    def remote(self, src, dst, slot, device):
        return pltpu.make_async_remote_copy(
            src_ref=src,
            dst_ref=dst,
            send_sem=self.send.at[slot],
            recv_sem=self.recv.at[slot],
            device_id=device,
            device_id_type=MESH,
        )


def layer_kernel(
    x_hbm, g_hbm, b_ref, c_ref, dt_ref, bias_ref, rate_ref, skip_ref, gain_ref, seg_ref, w_ref,
    out_ref,
    xv, gv, n_ref, ss_ref, inner, mask, products, spread, seg_own, seg_before,
    local_state, state_out, state_in, pair_out, pair_in, decay_own, decay_two,
    wf, nf, part, ring, fin_src, fin, sums, send, recv, local,
):
    seq, head = lax.axis_index("seq"), lax.axis_index("head")
    x, y = seq // YS, seq % YS
    z, c = head // 2, head % 2
    other = 1 - c

    def device(x_at, y_at, z_at, c_at):
        return {"seq": x_at * YS + y_at, "head": z_at * 2 + c_at}

    copies = Copies(send, recv)
    started = []

    def start(copy):
        copy.start()
        started.append(copy)
        return copy

    sibling = device(x, y, z, other)

    def weight_peer(step):
        return device(x, (y + step) % YS, z, c)

    def token_peer(step, core):
        return device((x + step) % XS, y, z, core)

    half = wf.shape[3] // 2
    rows = nf.shape[3]
    tokens, lanes = xv.shape[1], xv.shape[2]
    heads = dt_ref.shape[1]
    upper, lower = pl.ds(0, half), pl.ds(half, half)

    x_copy = pltpu.make_async_copy(x_hbm, xv, local.at[9])
    g_copy = pltpu.make_async_copy(g_hbm, gv, local.at[10])
    x_copy.start()

    def follower(distance):
        return {"seq": (seq + distance) % 16, "head": head}

    barrier = pltpu.get_barrier_semaphore()

    def greet(target):
        pl.semaphore_signal(barrier, inc=1, device_id=target, device_id_type=MESH)

    greet(sibling)
    for step in (1, -1):
        for core in (0, 1):
            greet(device((x + step + XS) % XS, y, z, core))
            greet(device(x, (y + step + YS) % YS, z, core))
        greet(device(x, y, (z + step + ZS) % ZS, c))
    for distance in (1, 2, 3):
        greet(follower(16 - distance))
    stays = jnp.logical_and(z % 2 == y // 2, c == y % 2)
    for core in (0, 1):
        pl.when(jnp.logical_not(jnp.logical_and(stays, c == core)))(
            functools.partial(
                greet, device(x, 2 * (z % 2) + c, 2 * (z // 2) + y // 2, core)
            )
        )
    for i in range(16):
        pl.when(jnp.logical_not(jnp.logical_and(seq == head, head == i)))(
            functools.partial(greet, {"seq": head, "head": i})
        )
    greeted = 32 - stays.astype(jnp.int32) - (seq == head).astype(jnp.int32)

    seg_row = seg_ref[...].astype(jnp.float32)
    seg_own[...] = jnp.broadcast_to(seg_row, seg_own.shape)

    arrived = {}
    size = YS
    own_local = []
    weight_slot = [copies.take(5) for model in (0, 1)]
    order = ((1, upper, 0), (-1, lower, 1), (1, lower, 2), (-1, upper, 3))

    def send_weights(model, which):
        at = y
        for step, part_rows, n in order:
            if n in which:
                copy = start(
                    copies.remote(
                        w_ref.at[model, part_rows],
                        wf.at[model, at, c, part_rows],
                        weight_slot[model] + n,
                        weight_peer(step),
                    )
                )
                arrived[model, n] = copy

    g_copy.start()
    forward_later = {}
    for model in (0, 1):
        at = y
        own = pltpu.make_async_copy(w_ref.at[model], wf.at[model, at, c], local.at[model])
        own.start()
        own_local.append(own)

    def share_own(model):
        forward_later[model] = start(
            copies.remote(
                w_ref.at[model],
                wf.at[model, y, c],
                weight_slot[model] + 4,
                sibling,
            )
        )

    row_at = lax.broadcasted_iota(jnp.int32, (tokens, tokens), 0)
    col_at = lax.broadcasted_iota(jnp.int32, (tokens, tokens), 1)
    eye = (row_at == col_at).astype(jnp.float32)
    lower_ones = (row_at >= col_at).astype(jnp.float32)
    seg_col = lax.dot_general(
        eye, seg_own[...], (((1,), (1,)), ((), ())), precision=highest
    )[:, 0:1]
    mask[...] = jnp.where(
        jnp.logical_and(row_at >= col_at, jnp.abs(seg_col - seg_row) < 0.5), 0.0, FAR
    )
    spread[...] = (
        lax.broadcasted_iota(jnp.int32, spread.shape, 0)
        == lax.broadcasted_iota(jnp.int32, spread.shape, 1) // (lanes // heads)
    ).astype(spread.dtype)
    same_last = (jnp.abs(seg_col - seg_row[:, tokens - 1 : tokens]) < 0.5).astype(jnp.float32)

    def widen(values, columns):
        coarse = values.astype(jnp.bfloat16)
        fine = (values - coarse.astype(jnp.float32)).astype(jnp.bfloat16)
        table = spread[:, columns]
        return jnp.dot(coarse, table, preferred_element_type=jnp.float32) + jnp.dot(
            fine, table, preferred_element_type=jnp.float32
        )

    blocks = [pl.ds(start_at, 256) for start_at in range(0, lanes, 256)]
    state_first = copies.take(2)
    state_copies, running, shifted, totals, tails = {}, {}, {}, {}, {}
    for model in (1, 0):
        raw = (
            lax.dot_general(eye, dt_ref[model], (((1,), (1,)), ((), ())), precision=highest)
            + bias_ref[model : model + 1, :]
        )
        step_size = jnp.maximum(raw, 0.0) + jnp.log1p(jnp.exp(-jnp.abs(raw)))
        log_decay = -(rate_ref[model : model + 1, :] * step_size)
        run = jnp.dot(lower_ones, log_decay, precision=highest)
        total = run[tokens - 1 : tokens, :]
        tails[model] = jnp.exp(total - run) * same_last * step_size
        running[model] = run
        totals[model] = total
        shifted[model] = run - jnp.log(step_size)
        seg_own[1 + model : 2 + model, 0:heads] = total

    def own_state(model):
        for block in blocks:
            weighted = (
                xv[model, :, block].astype(jnp.float32) * widen(tails[model], block)
            ).astype(jnp.bfloat16)
            fresh = lax.dot_general(
                b_ref[model],
                weighted,
                (((0,), (0,)), ((), ())),
                preferred_element_type=jnp.float32,
            )
            local_state[model, :, block] = fresh
            state_out[model, :, block] = fresh.astype(jnp.bfloat16)

    def send_state(model):
        state_copies[model] = start(
            copies.remote(
                state_out.at[model], state_in.at[model], state_first + model, follower(1)
            )
        )

    x_copy.wait()
    own_state(1)
    pl.semaphore_wait(barrier, greeted)
    info_first = copies.take(3)
    info_copies = [
        start(copies.remote(seg_own, seg_before.at[i], info_first + i, follower(i + 1)))
        for i in range(3)
    ]
    send_state(1)
    send_weights(1, (1,))
    own_state(0)
    send_state(0)
    share_own(1)
    share_own(0)

    for copy in info_copies:
        copy.wait_recv()

    def last_of(block_at):
        if block_at == 0:
            return seg_row[:, tokens - 1 : tokens]
        return seg_before[block_at - 1, 0:1, tokens - 1 : tokens]

    def decay_over(block_at, model, total):
        present = jnp.where(seq > block_at, 1.0, 0.0)
        same = (jnp.abs(last_of(block_at) - last_of(block_at + 1)) < 0.5).astype(jnp.float32)
        return jnp.exp(total) * same * present

    entered = (jnp.abs(seg_col - last_of(1)) < 0.5).astype(jnp.float32) * jnp.where(
        seq > 0, 1.0, 0.0
    )
    for model in (1, 0):
        near_decay = decay_over(0, model, totals[model])
        two = decay_over(1, model, seg_before[0, 1 + model : 2 + model, 0:heads]) * decay_over(
            2, model, seg_before[1, 1 + model : 2 + model, 0:heads]
        )
        for block in blocks:
            decay_own[model : model + 1, block] = widen(
                jnp.broadcast_to(near_decay, (8, heads)), block
            )[0:1, :]
            decay_two[model : model + 1, block] = widen(
                jnp.broadcast_to(two, (8, heads)), block
            )[0:1, :]

    def inside(model):
        run = running[model]
        shifted_t = lax.dot_general(
            shifted[model], eye, (((0,), (0,)), ((), ())), precision=highest
        )
        products[...] = lax.dot_general(
            c_ref[model],
            b_ref[model],
            (((1,), (1,)), ((), ())),
            preferred_element_type=jnp.float32,
        )
        lane = lax.broadcasted_iota(jnp.int32, (1, 128), 1)
        skip = jnp.broadcast_to(skip_ref[model : model + 1, :], (8, heads))
        mid = tokens // 2
        for pair in range(heads // 2):
            columns = pl.ds(128 * pair, 128)
            x_pair = xv[model, :, columns]
            early = late = None
            for q in (0, 1):
                h = 2 * pair + q
                x_one = x_pair * (lane // 64 == q).astype(jnp.bfloat16)
                gap = run[:mid, h : h + 1] - shifted_t[h : h + 1, :mid] + mask[:mid, :mid]
                weights = (jnp.exp(gap) * products[:mid, :mid]).astype(jnp.bfloat16)
                term = jnp.dot(weights, x_one[:mid], preferred_element_type=jnp.float32)
                early = term if early is None else early + term
                gap = run[mid:, h : h + 1] - shifted_t[h : h + 1, :] + mask[mid:, :]
                weights = (jnp.exp(gap) * products[mid:, :]).astype(jnp.bfloat16)
                term = jnp.dot(weights, x_one, preferred_element_type=jnp.float32)
                late = term if late is None else late + term
            passed = x_pair.astype(jnp.float32) * widen(skip, columns)[0:1, :]
            inner[model, :mid, columns] = early + passed[:mid]
            inner[model, mid:, columns] = late + passed[mid:]

    pair_first = copies.take(4)
    pair_copies = {}

    def join_pair(model):
        state_copies[model].wait_recv()
        for block in blocks:
            pair_out[model, :, block] = (
                local_state[model, :, block]
                + decay_own[model : model + 1, block] * state_in[model, :, block].astype(jnp.float32)
            ).astype(jnp.bfloat16)
        pair_copies[model] = [
            start(
                copies.remote(
                    pair_out.at[model],
                    pair_in.at[model, i],
                    pair_first + 2 * model + i,
                    follower(1 + 2 * i),
                )
            )
            for i in (1, 0)
        ]

    def gate(model):
        entry_w = jnp.exp(running[model]) * entered
        squares = jnp.zeros((tokens, 128), jnp.float32)
        for copy in pair_copies[model]:
            copy.wait_recv()
        for block in blocks:
            earlier = pair_in[model, 0, :, block].astype(jnp.float32) + decay_two[
                model : model + 1, block
            ] * pair_in[model, 1, :, block].astype(jnp.float32)
            entering = jnp.dot(
                c_ref[model], earlier.astype(jnp.bfloat16), preferred_element_type=jnp.float32
            )
            ssd_out = inner[model, :, block] + widen(entry_w, block) * entering
            opened = gv[model, :, block].astype(jnp.float32)
            gated = ssd_out * (opened / (1.0 + jnp.exp(-opened)))
            squares = squares + (
                gated[:, :128] * gated[:, :128] + gated[:, 128:] * gated[:, 128:]
            )
            n_ref[model, :, block] = (gated * gain_ref[model : model + 1, block]).astype(
                jnp.bfloat16
            )
        sums_row = lax.dot_general(
            jnp.ones((8, 128), jnp.float32),
            squares,
            (((1,), (1,)), ((), ())),
            precision=highest,
        )
        ss_ref[2 * model : 2 * model + 1, :] = sums_row[0:1, :128]
        ss_ref[2 * model + 1 : 2 * model + 2, :] = sums_row[0:1, 128:]

    inside(1)
    join_pair(1)
    inside(0)
    join_pair(0)
    send_weights(1, (3, 0, 2))
    send_weights(0, (0, 2))
    g_copy.wait()
    ss_ref[...] = jnp.zeros_like(ss_ref)

    token_in = {}
    token_own = {}

    def send_tokens(model):
        at = x
        mine = pl.ds(pl.multiple_of(c * rows, rows), rows)
        theirs = pl.ds(pl.multiple_of(other * rows, rows), rows)
        own = pltpu.make_async_copy(n_ref.at[model, mine], nf.at[model, c, at], local.at[3 + model])
        own.start()
        token_own[model] = own
        first = copies.take(8)
        to_sibling = start(
            copies.remote(n_ref.at[model, theirs], nf.at[model, c, at], first + 4, sibling)
        )
        sends = []
        for core in (0, 1):
            for n, step in ((0, 1), (1, -1)):
                piece = n_ref.at[model, pl.ds(core * rows, rows)]
                copy = pltpu.make_async_remote_copy(
                    src_ref=piece,
                    dst_ref=nf.at[model, c, at],
                    send_sem=send.at[first + 2 * core + n],
                    recv_sem=recv.at[first + 2 * c + n],
                    device_id=token_peer(step, core),
                    device_id_type=MESH,
                )
                sends.append(start(copy))
        token_in[model] = (first, to_sibling)

    def arrival(dst, slot):
        return copies.remote(dst, dst, slot, sibling)

    shared = {}
    onward = {1: (1, 3), 0: (0, 1)}

    def forward_weights(model, n):
        at = y
        step, part_rows = order[n][0], order[n][1]
        source = (at - step + size) % size
        arrived[model, n].wait_recv()
        held = wf.at[model, source, c, part_rows]
        if n in onward[model]:
            shared[model, n, "on"] = start(
                copies.remote(held, held, copies.take(), weight_peer(step))
            )
        shared[model, n, "near"] = start(copies.remote(held, held, copies.take(), sibling))

    def forward_opposite(model, n):
        part_rows = order[n][1]
        source = (y + 2) % size
        shared[model, n, "on"].wait_recv()
        held = wf.at[model, source, c, part_rows]
        shared[model, n, "far"] = start(copies.remote(held, held, copies.take(), sibling))

    token_forward = {}

    def forward_tokens(model):
        at = x
        first, to_sibling = token_in[model]
        forwards = []
        for core, n, step in ((0, 0, 1), (1, 1, -1), (1, 0, 1), (0, 1, -1)):
            source = (at - step + size) % size
            arrival(nf.at[model, core, source], first + 2 * core + n).wait_recv()
            if core == n:
                forwards.append(
                    start(
                        copies.remote(
                            nf.at[model, core, source],
                            nf.at[model, core, source],
                            first + 5 + n,
                            token_peer(step, c),
                        )
                    )
                )
        token_forward[model] = (to_sibling, forwards)

    forward_weights(1, 1)
    gate(1)
    send_tokens(1)
    gate(0)
    forward_weights(1, 3)
    send_weights(0, (1, 3))
    forward_tokens(1)
    send_tokens(0)
    sums_first = copies.take(16)
    sums_local = pltpu.make_async_copy(ss_ref, sums.at[head], local.at[2])
    sums_sent = []
    for i in range(16):
        copy = pltpu.make_async_remote_copy(
            src_ref=ss_ref,
            dst_ref=sums.at[head],
            send_sem=send.at[sums_first + i],
            recv_sem=recv.at[sums_first + head],
            device_id={"seq": (seq + i) % 16, "head": seq},
            device_id_type=MESH,
        )
        sums_sent.append(copy)
        if i == 0:
            pl.when(head != seq)(copy.start)
            pl.when(head == seq)(sums_local.start)
        else:
            copy.start()

    forward_weights(1, 0)
    forward_weights(1, 2)
    forward_opposite(1, 1)

    def piece(model, z_to, e):
        return part.at[model, (2 * (z_to % 2) + e - y + 4) % 4, z_to // 2]

    ring_first = copies.take(112)
    sent_ring = {}
    thin = rows // 4

    def ring_step(model, k, late):
        e = y % 2 if late else 1 - y % 2
        for v in (0, 1):
            for u, step in ((0, 1), (1, -1)):
                strip = pl.ds((2 * u + v) * thin, thin)
                z_to = (z - step * (1 + k) + 2 * ZS) % ZS
                if k == 0:
                    src = piece(model, z_to, e).at[strip]
                else:
                    sent_ring[model, late, u, v, k - 1].wait_recv()
                    src = ring.at[model, late, k - 1, strip]
                    src[...] = (
                        src[...].astype(jnp.float32)
                        + piece(model, z_to, e)[strip].astype(jnp.float32)
                    ).astype(src.dtype)
                sent_ring[model, late, u, v, k] = start(
                    copies.remote(
                        src,
                        ring.at[model, late, k, strip],
                        ring_first + 56 * model + 28 * late + 14 * u + 7 * v + k,
                        device(x, y, (z + step + ZS) % ZS, c),
                    )
                )

    def multiply(model, j, t):
        total = None
        for core in (0, 1):
            tokens = nf[model, core].reshape(4 * rows, nf.shape[4])
            term = jnp.dot(tokens, wf[model, j, core], preferred_element_type=jnp.float32)
            total = term if total is None else total + term
        part[model, t] = total.reshape(4, rows, total.shape[1]).astype(part.dtype)

    fin_first = copies.take(8)
    finals = []

    def finish(model):
        for late in (0, 1):
            e = y % 2 if late else 1 - y % 2
            for u in (0, 1):
                for v in (0, 1):
                    sent_ring[model, late, u, v, 6].wait_recv()
            fin_src[model, late] = (
                ring[model, late, 6].astype(jnp.float32)
                + piece(model, z, e)[...].astype(jnp.float32)
            ).astype(fin_src.dtype)
            target = device(x, 2 * (z % 2) + e, 2 * (z // 2) + y // 2, y % 2)
            copy = pltpu.make_async_remote_copy(
                src_ref=fin_src.at[model, late],
                dst_ref=fin.at[model, c],
                send_sem=send.at[fin_first + 4 * model + late],
                recv_sem=recv.at[fin_first + 4 * model + c],
                device_id=target,
                device_id_type=MESH,
            )
            if late:
                here = pltpu.make_async_copy(
                    fin_src.at[model, late], fin.at[model, c], local.at[5 + model]
                )
                pl.when(jnp.logical_not(stays))(copy.start)
                pl.when(stays)(here.start)
                finals.append(copy)
            else:
                start(copy)

    def tokens_ready(model):
        to_sibling, forwards = token_forward[model]
        token_own[model].wait()
        to_sibling.wait_recv()
        for copy in forwards:
            copy.wait_recv()

    def product(model, t):
        at = y
        if t == 0:
            own_local[model].wait()
            forward_later[model].wait_recv()
        elif t == 1:
            shared[model, 1, "near"].wait_recv()
            shared[model, 3, "near"].wait_recv()
        elif t == 3:
            shared[model, 0, "near"].wait_recv()
            shared[model, 2, "near"].wait_recv()
        else:
            for n in onward[model]:
                shared[model, n, "far"].wait_recv()
        multiply(model, (at + t) % 4, t)

    tokens_ready(1)
    product(1, 0)
    product(1, 1)
    product(1, 3)
    ring_step(1, 0, 0)
    forward_opposite(1, 3)
    ring_step(1, 1, 0)
    product(1, 2)
    ring_step(1, 0, 1)
    forward_weights(0, 0)
    ring_step(1, 2, 0)
    ring_step(1, 1, 1)
    forward_tokens(0)
    ring_step(1, 3, 0)
    ring_step(1, 2, 1)
    forward_weights(0, 1)
    ring_step(1, 4, 0)
    ring_step(1, 3, 1)
    forward_weights(0, 2)
    tokens_ready(0)
    product(0, 0)
    ring_step(1, 5, 0)
    ring_step(1, 4, 1)
    ring_step(1, 6, 0)
    ring_step(1, 5, 1)
    forward_weights(0, 3)
    product(0, 3)
    ring_step(1, 6, 1)
    product(0, 1)
    ring_step(0, 0, 0)
    finish(1)
    forward_opposite(0, 0)
    ring_step(0, 1, 0)
    ring_step(0, 2, 0)
    forward_opposite(0, 1)
    product(0, 2)
    ring_step(0, 0, 1)
    for k in range(3, 7):
        ring_step(0, k, 0)
        ring_step(0, k - 2, 1)
    ring_step(0, 5, 1)
    ring_step(0, 6, 1)

    for i in range(16):
        here = jnp.logical_and(seq == head, head == i)
        arrived = pltpu.make_async_remote_copy(
            src_ref=ss_ref,
            dst_ref=sums.at[i],
            send_sem=send.at[sums_first + i],
            recv_sem=recv.at[sums_first + i],
            device_id=sibling,
            device_id_type=MESH,
        )
        pl.when(here)(sums_local.wait)
        pl.when(jnp.logical_not(here))(arrived.wait_recv)
    mean_square = jnp.sum(sums[...], axis=0) / 16384.0
    scale = lax.rsqrt(mean_square + 1e-05)
    columns = jnp.concatenate([scale] * 16, axis=0).T

    finish(0)
    for model in (1, 0):
        for core in (0, 1):
            from_self = jnp.logical_and(stays, c == core)
            landed = copies.remote(
                fin_src.at[model, 0], fin.at[model, core], fin_first + 4 * model + core, sibling
            )
            pl.when(jnp.logical_not(from_self))(landed.wait_recv)

            @pl.when(from_self)
            def _():
                pltpu.make_async_copy(
                    fin_src.at[model, 0], fin.at[model, core], local.at[5 + model]
                ).wait()

            out_ref[model, core * rows : (core + 1) * rows] = (
                fin[model, core].astype(jnp.float32)
                * columns[:, 2 * model + core : 2 * model + core + 1]
            ).astype(out_ref.dtype)

    for copy in started:
        copy.wait_send()
    for i, copy in enumerate(sums_sent):
        if i == 0:
            pl.when(head != seq)(copy.wait_send)
        else:
            copy.wait_send()
    for copy in finals:
        pl.when(jnp.logical_not(stays))(copy.wait_send)


def local(
    x_heads, gate_z, b_proj, c_proj, dt_raw, dt_bias, decay_rate, skip_d, norm_gain, w_out, seg_ids
):
    tokens, lanes = x_heads.shape[1], x_heads.shape[2]
    depth, width = w_out.shape[1], w_out.shape[2]
    state, rows = b_proj.shape[2], tokens // 2
    bf16, f32 = jnp.bfloat16, jnp.float32
    vmem = pl.BlockSpec(memory_space=pltpu.VMEM)
    hbm = pl.BlockSpec(memory_space=pl.ANY)
    count = 232
    return pl.pallas_call(
        layer_kernel,
        out_shape=jax.ShapeDtypeStruct((2, tokens, width), bf16),
        in_specs=[hbm, hbm] + [vmem] * 8 + [hbm],
        out_specs=vmem,
        scratch_shapes=[
            pltpu.VMEM((2, tokens, lanes), bf16),
            pltpu.VMEM((2, tokens, lanes), bf16),
            pltpu.VMEM((2, tokens, lanes), bf16),
            pltpu.VMEM((8, 128), f32),
            pltpu.VMEM((2, tokens, lanes), f32),
            pltpu.VMEM((tokens, tokens), f32),
            pltpu.VMEM((tokens, tokens), f32),
            pltpu.VMEM((dt_raw.shape[2], lanes), bf16),
            pltpu.VMEM((8, tokens), f32),
            pltpu.VMEM((3, 8, tokens), f32),
            pltpu.VMEM((2, state, lanes), f32),
            pltpu.VMEM((2, state, lanes), bf16),
            pltpu.VMEM((2, state, lanes), bf16),
            pltpu.VMEM((2, state, lanes), bf16),
            pltpu.VMEM((2, 2, state, lanes), bf16),
            pltpu.VMEM((8, lanes), f32),
            pltpu.VMEM((8, lanes), f32),
            pltpu.VMEM((2, 4, 2, depth, width), bf16),
            pltpu.VMEM((2, 2, 4, rows, depth), bf16),
            pltpu.VMEM((2, 4, 4, rows, width), bf16),
            pltpu.VMEM((2, 2, 7, rows, width), bf16),
            pltpu.VMEM((2, 2, rows, width), bf16),
            pltpu.VMEM((2, 2, rows, width), bf16),
            pltpu.VMEM((16, 8, 128), f32),
            pltpu.SemaphoreType.DMA((count,)),
            pltpu.SemaphoreType.DMA((count,)),
            pltpu.SemaphoreType.DMA((11,)),
        ],
        compiler_params=pltpu.CompilerParams(
            collective_id=0, has_side_effects=True, vmem_limit_bytes=62 * 1024 * 1024
        ),
    )(
        x_heads,
        gate_z,
        b_proj,
        c_proj,
        jnp.transpose(dt_raw, (0, 2, 1)),
        dt_bias,
        decay_rate,
        skip_d,
        norm_gain,
        seg_ids.reshape(1, tokens),
        w_out,
    )


def solution(mesh):
    placed = (
        P(None, "seq", "head"),
        P(None, "seq", "head"),
        P(None, "seq", None),
        P(None, "seq", None),
        P(None, "seq", "head"),
        P(None, "head"),
        P(None, "head"),
        P(None, "head"),
        P(None, "head"),
        P(None, "head", "seq"),
        P("seq"),
    )
    return jax.shard_map(
        local, mesh=mesh, in_specs=placed, out_specs=P(None, "head", "seq"), check_vma=False
    )
```

time: 192 us -> 148 us (0.77)
  the two profiles are of different devices: /device:TPU:27 before, /device:TPU:41 now
where the time goes in v4:
time: 148 us; the launch traced here: 146 us
  Pallas kernels  145 us (98%)
  local copies, waits for them, and re-layouts  1.87 us (1%)
    pallas_call x1, Pallas kernels, local(): pl.pallas_call(layer_kernel, out_shape=jax.ShapeDtypeStruct((2, tokens, w...  145 us

profile of v4, /device:TPU:41, one launch (start us, length us, event | category | flops | bytes accessed | tf_op | source)
XLA Modules:
  0.0 146.5 jit_solution(1108975578726876296)
XLA Ops:
  0.0 144.6 %shard_map.109 = bf16[2,256,512]{2,1,0:T(8,128)(2,1)} custom-call(bf16[2,256,1024]{2,1,0:T(8,128)(2,1)} %x_hbm.1, bf16[2,256,1024]{2,1,0:T(8,128)(2,1)} %g_hbm.1, bf16[2,256,128]{2,1,0:T(8,128)(2,1)} %b_ref.1, bf16[2,256,128]{2,1,0:T(8,128)(2,1)} %c_ref.1, f32[2,16,256]{2,1,0:T(8,128)} %bitcast.2, f32[2,16]{1,0:T(2,128)} %bias_ref.1, f32[2,16]{1,0:T(2,128)} %rate_ref.1, ...), custom_call_target="tpu_custom_call" | custom-call | tf_op jit(solution)/shard_map/pallas_call | solution.py:650
  144.6 1.9 %copy.13 = bf16[2,256,512]{2,1,0:T(8,128)(2,1)} copy(bf16[2,256,512]{2,1,0:T(8,128)(2,1)} %shard_map.109) | data formatting | bytes 1048576

commit v5 on v4

--- a/solution.py
+++ b/solution.py
@@ -342,7 +342,6 @@
     inside(0)
     join_pair(0)
     send_weights(1, (3, 0, 2))
-    send_weights(0, (0, 2))
     g_copy.wait()
     ss_ref[...] = jnp.zeros_like(ss_ref)
 
@@ -379,7 +378,10 @@
         return copies.remote(dst, dst, slot, sibling)
 
     shared = {}
-    onward = {1: (1, 3), 0: (0, 1)}
+    onward = {
+        1: {1: lower, 3: pl.ds(half // 2, half // 2), 0: pl.ds(0, half // 2)},
+        0: {0: upper, 1: lower},
+    }
 
     def forward_weights(model, n):
         at = y
@@ -388,16 +390,16 @@
         arrived[model, n].wait_recv()
         held = wf.at[model, source, c, part_rows]
         if n in onward[model]:
+            passed = wf.at[model, source, c, onward[model][n]]
             shared[model, n, "on"] = start(
-                copies.remote(held, held, copies.take(), weight_peer(step))
+                copies.remote(passed, passed, copies.take(), weight_peer(step))
             )
         shared[model, n, "near"] = start(copies.remote(held, held, copies.take(), sibling))
 
     def forward_opposite(model, n):
-        part_rows = order[n][1]
         source = (y + 2) % size
         shared[model, n, "on"].wait_recv()
-        held = wf.at[model, source, c, part_rows]
+        held = wf.at[model, source, c, onward[model][n]]
         shared[model, n, "far"] = start(copies.remote(held, held, copies.take(), sibling))
 
     token_forward = {}
@@ -450,6 +452,7 @@
             copy.start()
 
     forward_weights(1, 0)
+    send_weights(0, (0, 2))
     forward_weights(1, 2)
     forward_opposite(1, 1)
 
@@ -460,29 +463,44 @@
     sent_ring = {}
     thin = rows // 4
 
-    def ring_step(model, k, late):
+    def ring_step(model, k, late, own=None):
         e = y % 2 if late else 1 - y % 2
+        moves = []
         for v in (0, 1):
             for u, step in ((0, 1), (1, -1)):
                 strip = pl.ds((2 * u + v) * thin, thin)
                 z_to = (z - step * (1 + k) + 2 * ZS) % ZS
-                if k == 0:
-                    src = piece(model, z_to, e).at[strip]
-                else:
-                    sent_ring[model, late, u, v, k - 1].wait_recv()
+                term = piece(model, z_to, e).at[strip]
+                previous, src = None, term
+                if k > 0:
+                    previous = sent_ring[model, late, u, v, k - 1]
                     src = ring.at[model, late, k - 1, strip]
+                copy = copies.remote(
+                    src,
+                    ring.at[model, late, k, strip],
+                    ring_first + 56 * model + 28 * late + 14 * u + 7 * v + k,
+                    device(x, y, (z + step + ZS) % ZS, c),
+                )
+                moves.append((previous, src, term, copy))
+                sent_ring[model, late, u, v, k] = copy
+                if own is not False:
+                    started.append(copy)
+
+        def move():
+            for previous, src, term, copy in moves:
+                if previous is not None:
+                    previous.wait_recv()
                     src[...] = (
-                        src[...].astype(jnp.float32)
-                        + piece(model, z_to, e)[strip].astype(jnp.float32)
+                        src[...].astype(jnp.float32) + term[...].astype(jnp.float32)
                     ).astype(src.dtype)
-                sent_ring[model, late, u, v, k] = start(
-                    copies.remote(
-                        src,
-                        ring.at[model, late, k, strip],
-                        ring_first + 56 * model + 28 * late + 14 * u + 7 * v + k,
-                        device(x, y, (z + step + ZS) % ZS, c),
-                    )
-                )
+                copy.start()
+
+        if own is None:
+            move()
+        elif own:
+            pl.when((z + 1 + k) % 2 == y // 2)(move)
+        else:
+            pl.when((z + 1 + k) % 2 != y // 2)(move)
 
     def multiply(model, j, t):
         total = None
@@ -492,37 +510,35 @@
             total = term if total is None else total + term
         part[model, t] = total.reshape(4, rows, total.shape[1]).astype(part.dtype)
 
-    fin_first = copies.take(8)
+    fin_first = copies.take(16)
     finals = []
 
-    def finish(model):
-        for late in (0, 1):
-            e = y % 2 if late else 1 - y % 2
-            for u in (0, 1):
-                for v in (0, 1):
-                    sent_ring[model, late, u, v, 6].wait_recv()
-            fin_src[model, late] = (
-                ring[model, late, 6].astype(jnp.float32)
-                + piece(model, z, e)[...].astype(jnp.float32)
-            ).astype(fin_src.dtype)
-            target = device(x, 2 * (z % 2) + e, 2 * (z // 2) + y // 2, y % 2)
-            copy = pltpu.make_async_remote_copy(
-                src_ref=fin_src.at[model, late],
-                dst_ref=fin.at[model, c],
-                send_sem=send.at[fin_first + 4 * model + late],
-                recv_sem=recv.at[fin_first + 4 * model + c],
-                device_id=target,
-                device_id_type=MESH,
-            )
-            if late:
-                here = pltpu.make_async_copy(
-                    fin_src.at[model, late], fin.at[model, c], local.at[5 + model]
-                )
-                pl.when(jnp.logical_not(stays))(copy.start)
-                pl.when(stays)(here.start)
-                finals.append(copy)
-            else:
-                start(copy)
+    def finish(model, late, u):
+        e = y % 2 if late else 1 - y % 2
+        for v in (0, 1):
+            sent_ring[model, late, u, v, 6].wait_recv()
+        strip = pl.ds(2 * u * thin, 2 * thin)
+        fin_src[model, late, strip] = (
+            ring[model, late, 6, strip].astype(jnp.float32)
+            + piece(model, z, e)[strip].astype(jnp.float32)
+        ).astype(fin_src.dtype)
+        src = fin_src.at[model, late, strip]
+        dst = fin.at[model, c, strip]
+        copy = pltpu.make_async_remote_copy(
+            src_ref=src,
+            dst_ref=dst,
+            send_sem=send.at[fin_first + 8 * model + 2 * late + u],
+            recv_sem=recv.at[fin_first + 8 * model + 2 * c + u],
+            device_id=device(x, 2 * (z % 2) + e, 2 * (z // 2) + y // 2, y % 2),
+            device_id_type=MESH,
+        )
+        if late:
+            here = pltpu.make_async_copy(src, dst, local.at[5 + 2 * model + u])
+            pl.when(jnp.logical_not(stays))(copy.start)
+            pl.when(stays)(here.start)
+            finals.append(copy)
+        else:
+            start(copy)
 
     def tokens_ready(model):
         to_sibling, forwards = token_forward[model]
@@ -553,6 +569,7 @@
     product(1, 3)
     ring_step(1, 0, 0)
     forward_opposite(1, 3)
+    forward_opposite(1, 0)
     ring_step(1, 1, 0)
     product(1, 2)
     ring_step(1, 0, 1)
@@ -577,18 +594,27 @@
     ring_step(1, 6, 1)
     product(0, 1)
     ring_step(0, 0, 0)
-    finish(1)
+    for u in (0, 1):
+        finish(1, 0, u)
+    ring_step(0, 0, 1, True)
+    ring_step(0, 1, 0)
+    for u in (0, 1):
+        finish(1, 1, u)
     forward_opposite(0, 0)
-    ring_step(0, 1, 0)
+    ring_step(0, 1, 1, True)
     ring_step(0, 2, 0)
     forward_opposite(0, 1)
+    ring_step(0, 2, 1, True)
     product(0, 2)
-    ring_step(0, 0, 1)
+    ring_step(0, 0, 1, False)
     for k in range(3, 7):
         ring_step(0, k, 0)
-        ring_step(0, k - 2, 1)
-    ring_step(0, 5, 1)
-    ring_step(0, 6, 1)
+        ring_step(0, k - 2, 1, False)
+        ring_step(0, k, 1, True)
+    for u in (0, 1):
+        finish(0, 0, u)
+    ring_step(0, 5, 1, False)
+    ring_step(0, 6, 1, False)
 
     for i in range(16):
         here = jnp.logical_and(seq == head, head == i)
@@ -606,21 +632,22 @@
     scale = lax.rsqrt(mean_square + 1e-05)
     columns = jnp.concatenate([scale] * 16, axis=0).T
 
-    finish(0)
+    for u in (0, 1):
+        finish(0, 1, u)
     for model in (1, 0):
         for core in (0, 1):
             from_self = jnp.logical_and(stays, c == core)
-            landed = copies.remote(
-                fin_src.at[model, 0], fin.at[model, core], fin_first + 4 * model + core, sibling
-            )
-            pl.when(jnp.logical_not(from_self))(landed.wait_recv)
-
-            @pl.when(from_self)
-            def _():
-                pltpu.make_async_copy(
-                    fin_src.at[model, 0], fin.at[model, core], local.at[5 + model]
-                ).wait()
-
+            for u in (0, 1):
+                strip = pl.ds(2 * u * thin, 2 * thin)
+                dst = fin.at[model, core, strip]
+                landed = copies.remote(
+                    dst, dst, fin_first + 8 * model + 2 * core + u, sibling
+                )
+                kept_here = pltpu.make_async_copy(
+                    fin_src.at[model, 1, strip], dst, local.at[5 + 2 * model + u]
+                )
+                pl.when(jnp.logical_not(from_self))(landed.wait_recv)
+                pl.when(from_self)(kept_here.wait)
             out_ref[model, core * rows : (core + 1) * rows] = (
                 fin[model, core].astype(jnp.float32)
                 * columns[:, 2 * model + core : 2 * model + core + 1]
@@ -646,7 +673,7 @@
     bf16, f32 = jnp.bfloat16, jnp.float32
     vmem = pl.BlockSpec(memory_space=pltpu.VMEM)
     hbm = pl.BlockSpec(memory_space=pl.ANY)
-    count = 232
+    count = 248
     return pl.pallas_call(
         layer_kernel,
         out_shape=jax.ShapeDtypeStruct((2, tokens, width), bf16),

time: 148 us -> 151 us (1.020)
  the two profiles are of different devices: /device:TPU:41 before, /device:TPU:22 now
where the time goes in v5:
time: 151 us
  Pallas kernels  149 us (99%)
  local copies, waits for them, and re-layouts  1.87 us (1%)
    pallas_call x1, Pallas kernels, local(): pl.pallas_call(layer_kernel, out_shape=jax.ShapeDtypeStruct((2, tokens, w...  149 us

profile of v5, /device:TPU:22, one launch (start us, length us, event | category | flops | bytes accessed | tf_op | source)
XLA Modules:
  0.0 151.0 jit_solution(10864229879161317767)
XLA Ops:
  0.0 149.1 %shard_map.109 = bf16[2,256,512]{2,1,0:T(8,128)(2,1)} custom-call(bf16[2,256,1024]{2,1,0:T(8,128)(2,1)} %x_hbm.1, bf16[2,256,1024]{2,1,0:T(8,128)(2,1)} %g_hbm.1, bf16[2,256,128]{2,1,0:T(8,128)(2,1)} %b_ref.1, bf16[2,256,128]{2,1,0:T(8,128)(2,1)} %c_ref.1, f32[2,16,256]{2,1,0:T(8,128)} %bitcast.2, f32[2,16]{1,0:T(2,128)} %bias_ref.1, f32[2,16]{1,0:T(2,128)} %rate_ref.1, ...), custom_call_target="tpu_custom_call" | custom-call | tf_op jit(solution)/shard_map/pallas_call | solution.py:677
  149.1 1.9 %copy.13 = bf16[2,256,512]{2,1,0:T(8,128)(2,1)} copy(bf16[2,256,512]{2,1,0:T(8,128)(2,1)} %shard_map.109) | data formatting | bytes 1048576

commit v6 on v5

--- a/solution.py
+++ b/solution.py
@@ -573,20 +573,20 @@
     ring_step(1, 1, 0)
     product(1, 2)
     ring_step(1, 0, 1)
-    forward_weights(0, 0)
     ring_step(1, 2, 0)
     ring_step(1, 1, 1)
     forward_tokens(0)
     ring_step(1, 3, 0)
     ring_step(1, 2, 1)
-    forward_weights(0, 1)
+    forward_weights(0, 0)
     ring_step(1, 4, 0)
     ring_step(1, 3, 1)
+    forward_weights(0, 1)
+    ring_step(1, 5, 0)
+    ring_step(1, 4, 1)
     forward_weights(0, 2)
     tokens_ready(0)
     product(0, 0)
-    ring_step(1, 5, 0)
-    ring_step(1, 4, 1)
     ring_step(1, 6, 0)
     ring_step(1, 5, 1)
     forward_weights(0, 3)
@@ -594,26 +594,26 @@
     ring_step(1, 6, 1)
     product(0, 1)
     ring_step(0, 0, 0)
+    ring_step(0, 0, 1, True)
+    forward_opposite(0, 0)
+    ring_step(0, 1, 0)
+    ring_step(0, 1, 1, True)
     for u in (0, 1):
         finish(1, 0, u)
-    ring_step(0, 0, 1, True)
-    ring_step(0, 1, 0)
+    forward_opposite(0, 1)
+    ring_step(0, 2, 0)
+    product(0, 2)
+    ring_step(0, 0, 1, False)
+    ring_step(0, 2, 1, True)
+    ring_step(0, 1, 1, False)
     for u in (0, 1):
         finish(1, 1, u)
-    forward_opposite(0, 0)
-    ring_step(0, 1, 1, True)
-    ring_step(0, 2, 0)
-    forward_opposite(0, 1)
-    ring_step(0, 2, 1, True)
-    product(0, 2)
-    ring_step(0, 0, 1, False)
     for k in range(3, 7):
         ring_step(0, k, 0)
-        ring_step(0, k - 2, 1, False)
+        ring_step(0, k - 1, 1, False)
         ring_step(0, k, 1, True)
     for u in (0, 1):
         finish(0, 0, u)
-    ring_step(0, 5, 1, False)
     ring_step(0, 6, 1, False)
 
     for i in range(16):

time: 151 us -> 145 us (0.960)
  the two profiles are of different devices: /device:TPU:22 before, /device:TPU:41 now
where the time goes in v6:
time: 145 us
  Pallas kernels  143 us (99%)
  local copies, waits for them, and re-layouts  1.87 us (1%)
    pallas_call x1, Pallas kernels, local(): pl.pallas_call(layer_kernel, out_shape=jax.ShapeDtypeStruct((2, tokens, w...  143 us

profile of v6, /device:TPU:41, one launch (start us, length us, event | category | flops | bytes accessed | tf_op | source)
XLA Modules:
  0.0 144.6 jit_solution(812698435366850624)
XLA Ops:
  0.0 142.7 %shard_map.109 = bf16[2,256,512]{2,1,0:T(8,128)(2,1)} custom-call(bf16[2,256,1024]{2,1,0:T(8,128)(2,1)} %x_hbm.1, bf16[2,256,1024]{2,1,0:T(8,128)(2,1)} %g_hbm.1, bf16[2,256,128]{2,1,0:T(8,128)(2,1)} %b_ref.1, bf16[2,256,128]{2,1,0:T(8,128)(2,1)} %c_ref.1, f32[2,16,256]{2,1,0:T(8,128)} %bitcast.2, f32[2,16]{1,0:T(2,128)} %bias_ref.1, f32[2,16]{1,0:T(2,128)} %rate_ref.1, ...), custom_call_target="tpu_custom_call" | custom-call | tf_op jit(solution)/shard_map/pallas_call | solution.py:677
  142.7 1.9 %copy.13 = bf16[2,256,512]{2,1,0:T(8,128)(2,1)} copy(bf16[2,256,512]{2,1,0:T(8,128)(2,1)} %shard_map.109) | data formatting | bytes 1048576

commit v7 on v6

--- a/solution.py
+++ b/solution.py
@@ -9,6 +9,7 @@
 
 highest = lax.Precision.HIGHEST
 FAR = -1e30
+RING_AT = 85
 
 MESH = pl.DeviceIdType.MESH
 XS, YS, ZS = 4, 4, 8
@@ -16,18 +17,19 @@
 
 class Copies:
     def __init__(self, send, recv):
-        self.send, self.recv, self.used = send, recv, 0
-
-    def take(self, count=1):
+        self.send, self.recv, self.used, self.sends = send, recv, 0, 0
+
+    def take(self, count=1, sends=None):
         first = self.used
         self.used += count
+        self.sends += count if sends is None else sends
         return first
 
-    def remote(self, src, dst, slot, device):
+    def remote(self, src, dst, slot, device, send_slot=None):
         return pltpu.make_async_remote_copy(
             src_ref=src,
             dst_ref=dst,
-            send_sem=self.send.at[slot],
+            send_sem=self.send.at[slot if send_slot is None else send_slot],
             recv_sem=self.recv.at[slot],
             device_id=device,
             device_id_type=MESH,
@@ -459,7 +461,7 @@
     def piece(model, z_to, e):
         return part.at[model, (2 * (z_to % 2) + e - y + 4) % 4, z_to // 2]
 
-    ring_first = copies.take(112)
+    ring_first, ring_sends = RING_AT, RING_AT
     sent_ring = {}
     thin = rows // 4
 
@@ -480,11 +482,10 @@
                     ring.at[model, late, k, strip],
                     ring_first + 56 * model + 28 * late + 14 * u + 7 * v + k,
                     device(x, y, (z + step + ZS) % ZS, c),
+                    ring_sends + 2 * model + late,
                 )
                 moves.append((previous, src, term, copy))
                 sent_ring[model, late, u, v, k] = copy
-                if own is not False:
-                    started.append(copy)
 
         def move():
             for previous, src, term, copy in moves:
@@ -565,53 +566,62 @@
 
     tokens_ready(1)
     product(1, 0)
+    ring_step(1, 0, 1, True)
     product(1, 1)
     product(1, 3)
     ring_step(1, 0, 0)
+    ring_step(1, 1, 1, True)
     forward_opposite(1, 3)
     forward_opposite(1, 0)
     ring_step(1, 1, 0)
+    ring_step(1, 2, 1, True)
     product(1, 2)
-    ring_step(1, 0, 1)
+    ring_step(1, 0, 1, False)
     ring_step(1, 2, 0)
-    ring_step(1, 1, 1)
+    ring_step(1, 3, 1, True)
+    ring_step(1, 1, 1, False)
     forward_tokens(0)
     ring_step(1, 3, 0)
-    ring_step(1, 2, 1)
+    ring_step(1, 4, 1, True)
+    ring_step(1, 2, 1, False)
     forward_weights(0, 0)
     ring_step(1, 4, 0)
-    ring_step(1, 3, 1)
+    ring_step(1, 5, 1, True)
+    ring_step(1, 3, 1, False)
     forward_weights(0, 1)
     ring_step(1, 5, 0)
-    ring_step(1, 4, 1)
+    ring_step(1, 6, 1, True)
+    ring_step(1, 4, 1, False)
     forward_weights(0, 2)
     tokens_ready(0)
     product(0, 0)
+    ring_step(0, 0, 1, True)
     ring_step(1, 6, 0)
-    ring_step(1, 5, 1)
+    ring_step(1, 5, 1, False)
     forward_weights(0, 3)
+    for u in (0, 1):
+        finish(1, 0, u)
     product(0, 3)
-    ring_step(1, 6, 1)
+    ring_step(0, 1, 1, True)
     product(0, 1)
     ring_step(0, 0, 0)
-    ring_step(0, 0, 1, True)
+    ring_step(1, 6, 1, False)
+    ring_step(0, 2, 1, True)
     forward_opposite(0, 0)
+    for u in (0, 1):
+        finish(1, 1, u)
     ring_step(0, 1, 0)
-    ring_step(0, 1, 1, True)
-    for u in (0, 1):
-        finish(1, 0, u)
     forward_opposite(0, 1)
     ring_step(0, 2, 0)
     product(0, 2)
     ring_step(0, 0, 1, False)
-    ring_step(0, 2, 1, True)
+    ring_step(0, 3, 1, True)
     ring_step(0, 1, 1, False)
-    for u in (0, 1):
-        finish(1, 1, u)
     for k in range(3, 7):
         ring_step(0, k, 0)
         ring_step(0, k - 1, 1, False)
-        ring_step(0, k, 1, True)
+        if k < 6:
+            ring_step(0, k + 1, 1, True)
     for u in (0, 1):
         finish(0, 0, u)
     ring_step(0, 6, 1, False)
@@ -655,6 +665,13 @@
 
     for copy in started:
         copy.wait_send()
+    for model in (0, 1):
+        for late in (0, 1):
+            whole = ring.at[model, late]
+            copies.remote(
+                whole, whole, ring_first, sibling, ring_sends + 2 * model + late
+            ).wait_send()
+    assert copies.used <= RING_AT
     for i, copy in enumerate(sums_sent):
         if i == 0:
             pl.when(head != seq)(copy.wait_send)
@@ -673,7 +690,6 @@
     bf16, f32 = jnp.bfloat16, jnp.float32
     vmem = pl.BlockSpec(memory_space=pltpu.VMEM)
     hbm = pl.BlockSpec(memory_space=pl.ANY)
-    count = 248
     return pl.pallas_call(
         layer_kernel,
         out_shape=jax.ShapeDtypeStruct((2, tokens, width), bf16),
@@ -704,8 +720,8 @@
             pltpu.VMEM((2, 2, rows, width), bf16),
             pltpu.VMEM((2, 2, rows, width), bf16),
             pltpu.VMEM((16, 8, 128), f32),
-            pltpu.SemaphoreType.DMA((count,)),
-            pltpu.SemaphoreType.DMA((count,)),
+            pltpu.SemaphoreType.DMA((RING_AT + 4,)),
+            pltpu.SemaphoreType.DMA((RING_AT + 112,)),
             pltpu.SemaphoreType.DMA((11,)),
         ],
         compiler_params=pltpu.CompilerParams(

time: 145 us -> 148 us (1.021); the launches traced: 145 us -> 146 us
  no operation moved by 1% of the time
where the time goes in v7:
time: 148 us; the launch traced here: 146 us
  Pallas kernels  144 us (97%)
  local copies, waits for them, and re-layouts  1.87 us (1%)
    pallas_call x1, Pallas kernels, local(): pl.pallas_call(layer_kernel, out_shape=jax.ShapeDtypeStruct((2, tokens, w...  144 us

profile of v7, /device:TPU:41, one launch (start us, length us, event | category | flops | bytes accessed | tf_op | source)
XLA Modules:
  0.0 145.9 jit_solution(5049691967517209989)
XLA Ops:
  0.0 144.0 %shard_map.109 = bf16[2,256,512]{2,1,0:T(8,128)(2,1)} custom-call(bf16[2,256,1024]{2,1,0:T(8,128)(2,1)} %x_hbm.1, bf16[2,256,1024]{2,1,0:T(8,128)(2,1)} %g_hbm.1, bf16[2,256,128]{2,1,0:T(8,128)(2,1)} %b_ref.1, bf16[2,256,128]{2,1,0:T(8,128)(2,1)} %c_ref.1, f32[2,16,256]{2,1,0:T(8,128)} %bitcast.2, f32[2,16]{1,0:T(2,128)} %bias_ref.1, f32[2,16]{1,0:T(2,128)} %rate_ref.1, ...), custom_call_target="tpu_custom_call" | custom-call | tf_op jit(solution)/shard_map/pallas_call | solution.py:693
  144.0 1.9 %copy.13 = bf16[2,256,512]{2,1,0:T(8,128)(2,1)} copy(bf16[2,256,512]{2,1,0:T(8,128)(2,1)} %shard_map.109) | data formatting | bytes 1048576

commit v8 on v7

--- a/solution.py
+++ b/solution.py
@@ -599,24 +599,24 @@
     ring_step(1, 6, 0)
     ring_step(1, 5, 1, False)
     forward_weights(0, 3)
-    for u in (0, 1):
-        finish(1, 0, u)
     product(0, 3)
     ring_step(0, 1, 1, True)
     product(0, 1)
     ring_step(0, 0, 0)
     ring_step(1, 6, 1, False)
+    forward_opposite(0, 0)
     ring_step(0, 2, 1, True)
-    forward_opposite(0, 0)
+    ring_step(0, 1, 0)
     for u in (0, 1):
-        finish(1, 1, u)
-    ring_step(0, 1, 0)
+        finish(1, 0, u)
     forward_opposite(0, 1)
     ring_step(0, 2, 0)
     product(0, 2)
     ring_step(0, 0, 1, False)
     ring_step(0, 3, 1, True)
     ring_step(0, 1, 1, False)
+    for u in (0, 1):
+        finish(1, 1, u)
     for k in range(3, 7):
         ring_step(0, k, 0)
         ring_step(0, k - 1, 1, False)

time: 148 us -> 142 us (0.959); the launches traced: 146 us -> 142 us
  Pallas kernels: 144 us -> 140 us
    pallas_call x1, Pallas kernels: 144 us -> 140 us  [local(): pl.pallas_call(layer_kernel, out_shape=jax.ShapeDtypeStruct((2, tokens, w...]
where the time goes in v8:
time: 142 us
  Pallas kernels  140 us (99%)
  local copies, waits for them, and re-layouts  1.87 us (1%)
    pallas_call x1, Pallas kernels, local(): pl.pallas_call(layer_kernel, out_shape=jax.ShapeDtypeStruct((2, tokens, w...  140 us

profile of v8, /device:TPU:41, one launch (start us, length us, event | category | flops | bytes accessed | tf_op | source)
XLA Modules:
  0.0 141.9 jit_solution(14640827692049238928)
XLA Ops:
  0.0 140.1 %shard_map.109 = bf16[2,256,512]{2,1,0:T(8,128)(2,1)} custom-call(bf16[2,256,1024]{2,1,0:T(8,128)(2,1)} %x_hbm.1, bf16[2,256,1024]{2,1,0:T(8,128)(2,1)} %g_hbm.1, bf16[2,256,128]{2,1,0:T(8,128)(2,1)} %b_ref.1, bf16[2,256,128]{2,1,0:T(8,128)(2,1)} %c_ref.1, f32[2,16,256]{2,1,0:T(8,128)} %bitcast.2, f32[2,16]{1,0:T(2,128)} %bias_ref.1, f32[2,16]{1,0:T(2,128)} %rate_ref.1, ...), custom_call_target="tpu_custom_call" | custom-call | tf_op jit(solution)/shard_map/pallas_call | solution.py:693
  140.1 1.9 %copy.13 = bf16[2,256,512]{2,1,0:T(8,128)(2,1)} copy(bf16[2,256,512]{2,1,0:T(8,128)(2,1)} %shard_map.109) | data formatting | bytes 1048576
